TPU v7x, 128 devices: a whole 4x4x4 slice. The times are simulated.
128 devices in a mesh: row: 16 (over x, y), col: 8 (over z, core).
Axes of the slice: x: 4, y: 4, z: 4, core: 2. Of those that a mesh axis runs over, the one named last changes fastest.
Arguments:
- right_side: float32 [2, 128, 98304], P(None, None, ('row', 'col')), may hold values from -100 to 100
- self_impedance: float32 [2, 98304], P(None, ('row', 'col')), may hold values from -1 to 6, as said below
- near_blocks: bfloat16 [16, 48, 6, 2, 128, 128], P('row', 'col'), may hold values from -0.109375 to 0.109375
- near_columns: int32 [16, 48, 6], P('row', 'col'), may hold values from 0 to 47, as said below
- column_factors: bfloat16 [16, 16, 2, 64, 6144], P('row', None, None, None, 'col'), may hold values from -0.078125 to 0.078125
- row_factors: bfloat16 [16, 16, 2, 64, 6144], P('row', None, None, None, 'col'), may hold values from -0.15625 to 0.15625
- tile_ranks: int32 [16, 16], replicated, may hold values from 0 to 64, as said below
Outputs:
- solution: float32 [2, 128, 98304], P(None, None, ('row', 'col'))
- residual: float32 [2, 128, 98304], P(None, None, ('row', 'col'))
Inputs may be any that keep to these rules, and one draw needn't show every extreme that they name: `self_impedance`: real parts (index 0) lie between 4 and 6, imaginary parts between -1 and 1. `near_columns`: entry [r, p, s] is a column sub-block of block r within 2 sub-blocks of row sub-block p; slot 0 holds max(p - 2, 0) and slot 1 holds min(p + 2, 47). `tile_ranks`: zero on the diagonal tiles and from 16 to 64 on all others; both 16 and 64 occur.
All inputs are finite; a program needn't handle non-finite values.
Results may differ from a plain program's by a relative error of at most 0.015.
Values may be sent and summed in bfloat16 or wider, within the bound.
No kernel may reach another device: no remote copies, remote signals or barrier semaphores. Data moves between devices by JAX's collectives and lax.ppermute only.
A program may use at most 128 MiB of HBM per device.

v0:
```python
import jax
import jax.numpy as jnp
from jax import lax
from jax.experimental import pallas as pl
from jax.experimental.pallas import tpu as pltpu
from jax.sharding import Mesh, PartitionSpec as P


K = 64
SB = 128
HALO = 2
R = 128
TILES = 16
SLOTS = 6
SHIFT = 5.0

TOP = lax.Precision.HIGHEST
ALL = ("x", "y", "z", "c")
VMEM = pltpu.VMEM
SMEM = pl.BlockSpec(memory_space=pltpu.SMEM)
ANY = pl.BlockSpec(memory_space=pl.ANY)
WHOLE = pl.BlockSpec(memory_space=pltpu.VMEM)
SMALL, LARGE = 12 * 2**20, 60 * 1024 * 1024


def dot(a, b, over=(1, 0), precision=TOP):
    dims = (((over[0],), (over[1],)), ((), ()))
    return lax.dot_general(a, b, dims, precision=precision, preferred_element_type=jnp.float32)


def bf16_dot(a, b, over=(1, 0)):
    return dot(a, b, over, None)


def inverse_factor(gram):
    lane = lax.broadcasted_iota(jnp.int32, (8, R), 1)
    sub = lax.broadcasted_iota(jnp.int32, (8, R), 0)
    chunks = [gram[8 * j : 8 * j + 8] for j in range(R // 8)]
    floor = jnp.zeros((1, R), jnp.float32)
    for j in range(R // 8):
        floor = floor + jnp.sum(jnp.where(lane == sub + 8 * j, chunks[j], 0.0), axis=0, keepdims=True)
    floor = floor * 1e-7

    def full(x):
        return jnp.broadcast_to(x, (8, R))

    finished = []
    for j in range(R // 8):
        start = 8 * j
        inside = (lane >= start) & (lane < start + 8)
        rows = [full(chunks[j][t : t + 1]) for t in range(8)]
        pivots = [[full(rows[t][:, start + u : start + u + 1]) for u in range(8)] for t in range(8)]
        least = [full(floor[:, start + t : start + t + 1]) for t in range(8)]
        rows = [jnp.where(inside, jnp.where(lane == start + t, 1.0, 0.0), rows[t]) for t in range(8)]
        inverse = [None] * 8
        unit = [[None] * 8 for _ in range(8)]
        for t in range(8):
            pivots[t][t] = jnp.maximum(pivots[t][t], least[t])
            inverse[t] = 1.0 / pivots[t][t]
            for u in range(t + 1, 8):
                factor = pivots[t][u] * inverse[t]
                rows[u] = rows[u] - factor * rows[t]
                for s in range(t):
                    unit[u][s] = unit[u][s] - factor * unit[t][s]
                unit[u][t] = -factor
                for v in range(u, 8):
                    pivots[u][v] = pivots[u][v] - factor * pivots[t][v]
        done = jnp.zeros((8, R), jnp.float32)
        for t in range(8):
            done = jnp.where(sub == t, rows[t] * lax.rsqrt(pivots[t][t]), done)
        finished.append(jnp.where(lane <= sub + start, done, 0.0))
        solved = []
        for t in range(8):
            total = rows[t] * inverse[t]
            for u in range(t + 1, 8):
                total = total + (unit[u][t] * inverse[u]) * rows[u]
            solved.append(total)
        for i in range(j + 1, R // 8):
            chunk = chunks[i]
            terms = [chunk[:, start + t : start + t + 1] * solved[t] for t in range(8)]
            while len(terms) > 1:
                terms = [p + q for p, q in zip(terms[::2], terms[1::2])]
            chunks[i] = jnp.where(inside, 0.0, chunk) - terms[0]
    return jnp.concatenate(finished, axis=0)


class Copies:
    def __init__(self, sems):
        self.sems, self.count = sems, 0

    def start(self, source, target):
        copy = pltpu.make_async_copy(source, target, self.sems.at[self.count])
        self.count += 1
        copy.start()
        return copy


def wait(copies):
    for copy in copies:
        copy.wait()


def aligned(index, size):
    return pl.ds(pl.multiple_of(index * size, size), size)


def column_products(copies, x, columns, out, out_ref):
    flat = x.reshape(2 * R, x.shape[2])
    sign = jnp.where(lax.broadcasted_iota(jnp.int32, (R, 2 * K), 1) < K, -1.0, 1.0)
    sent = []
    for i in range(TILES):
        both = bf16_dot(flat, columns[2 * K * i : 2 * K * (i + 1)], (1, 1))
        out[i] = (both[:R] + sign * pltpu.roll(both[R:], K, 1)).astype(jnp.bfloat16)
        if i % 4 == 3:
            sent.append(copies.start(out.at[i - 3 : i + 1], out_ref.at[i - 3 : i + 1]))
    return sent


def send_basis(copies, basis, rounded, basis_ref, rounded_ref, low_ref, high_ref):
    width = basis.shape[2]
    return [
        copies.start(rounded.at[:, :, : HALO * SB], low_ref),
        copies.start(rounded.at[:, :, width - HALO * SB :], high_ref),
        copies.start(rounded, rounded_ref),
        copies.start(basis, basis_ref),
    ]


def gram_kernel(place_ref, side_ref, out_ref, whole):
    whole[...] = dot(side_ref[0], side_ref[0], (1, 1)) + dot(side_ref[1], side_ref[1], (1, 1))
    core = place_ref[1]
    for d in range(2):
        out_ref[d] = whole[aligned(core ^ d, R // 2)]


def start_kernel(
    place_ref, mine_ref, other_ref, side_ref, columns_ref, basis_ref, rounded_ref, low_ref, high_ref, out_ref,
    gram, side, columns, basis, rounded, out, sems,
):
    copies = Copies(sems)
    core = place_ref[1]
    side_copy = copies.start(side_ref, side)
    columns_copy = copies.start(columns_ref, columns)
    gram[aligned(core, R // 2)] = mine_ref[...]
    gram[aligned(1 - core, R // 2)] = other_ref[...]
    factor = inverse_factor(gram[...])
    side_copy.wait()
    for part in range(2):
        basis[part] = dot(factor, side[part])
    x = basis[...].astype(jnp.bfloat16)
    rounded[...] = x
    sent = send_basis(copies, basis, rounded, basis_ref, rounded_ref, low_ref, high_ref)
    columns_copy.wait()
    sent += column_products(copies, x, columns, out, out_ref)
    wait(sent)


def near_kernel(
    where_ref, x_ref, rounded_ref, low_ref, high_ref, self_ref, near_ref, out_ref,
    x, wide, impedance, near, picked, out, sems,
):
    copies = Copies(sems)
    width = x.shape[2]
    edge = HALO * SB
    first = [
        copies.start(low_ref, wide.at[:, :, :edge]),
        copies.start(rounded_ref, wide.at[:, :, edge : edge + width]),
        copies.start(high_ref, wide.at[:, :, edge + width :]),
        copies.start(self_ref, impedance),
    ]
    second = [copies.start(near_ref, near), copies.start(x_ref, x)]
    wait(first)
    impedance[0:1] = impedance[0:1] - SHIFT
    wait(second)

    def one(p, carry):
        for s in range(SLOTS):
            at = aligned(where_ref[p, s], SB)
            picked[:R, s * SB : (s + 1) * SB] = wide[0, :, at]
            picked[R:, s * SB : (s + 1) * SB] = wide[1, :, at]
        by_real = bf16_dot(picked[...], near[p, :, 0].reshape(SLOTS * SB, SB))
        by_imag = bf16_dot(picked[...], near[p, :, 1].reshape(SLOTS * SB, SB))
        at = aligned(p, SB)
        x_real, x_imag = x[0, :, at], x[1, :, at]
        re, im = impedance[0:1, at], impedance[1:2, at]
        out[0, :, at] = re * x_real - im * x_imag + (by_real[:R] - by_imag[R:])
        out[1, :, at] = re * x_imag + im * x_real + (by_imag[:R] + by_real[R:])
        return carry

    lax.fori_loop(0, near.shape[0], one, 0)
    copies.start(out, out_ref).wait()


def place_tiles(place_ref, own_ref, partner_ref, tiles):
    z, core = place_ref[0], place_ref[1]
    for k in range(4):
        chunk = 2 * (z ^ k)
        tiles[:, aligned(chunk + core, 16)] = own_ref[k]
        tiles[:, aligned(chunk + 1 - core, 16)] = partner_ref[k]


def far_part(place_ref, ranks_ref, own_ref, partner_ref, rows, tiles, left):
    place_tiles(place_ref, own_ref, partner_ref, tiles)
    lane = lax.broadcasted_iota(jnp.int32, (R, 2 * K), 1)
    rank = jnp.where(lane < K, lane, lane - K)
    sign = jnp.where(lane < K, 1.0, -1.0)
    for j in range(TILES):
        tile = jnp.where(rank < ranks_ref[j], tiles[j].astype(jnp.float32), 0.0)
        at = slice(2 * K * j, 2 * K * (j + 1))
        left[:R, at] = (tile * sign).astype(jnp.bfloat16)
        left[R:, at] = pltpu.roll(tile, K, 1).astype(jnp.bfloat16)
    return bf16_dot(left[...], rows[...]).reshape(2, R, rows.shape[1])


def middle_kernel(
    place_ref, ranks_ref, own_ref, partner_ref, rows, base_ref, columns_ref,
    basis_ref, rounded_ref, low_ref, high_ref, out_ref,
    tiles, left, columns, basis, rounded, out, sems,
):
    copies = Copies(sems)
    base_copy = copies.start(base_ref, basis)
    columns_copy = copies.start(columns_ref, columns)
    far = far_part(place_ref, ranks_ref, own_ref, partner_ref, rows, tiles, left)
    base_copy.wait()
    basis[...] = basis[...] + far
    x = basis[...].astype(jnp.bfloat16)
    rounded[...] = x
    sent = send_basis(copies, basis, rounded, basis_ref, rounded_ref, low_ref, high_ref)
    columns_copy.wait()
    sent += column_products(copies, x, columns, out, out_ref)
    wait(sent)


def last_kernel(
    place_ref, ranks_ref, own_ref, partner_ref, rows, base_ref, side_ref, basis_0_ref, basis_1_ref,
    basis_2_ref, sums_ref, tiles, left, basis, images, sums, sems,
):
    copies = Copies(sems)
    others = [copies.start(ref, basis.at[i]) for i, ref in enumerate((basis_0_ref, basis_1_ref, base_ref))]
    others += [copies.start(side_ref.at[part], images.at[part, :R]) for part in range(2)]
    far = far_part(place_ref, ranks_ref, own_ref, partner_ref, rows, tiles, left)
    wait(others)
    basis[2] = basis[2] + far
    sent = [copies.start(basis.at[2], basis_2_ref)]
    for j in range(2):
        for part in range(2):
            images[part, R * (j + 1) : R * (j + 2)] = basis[j + 1, part] + SHIFT * basis[j, part]
    total = [dot(images[part, R:], images[part, : 2 * R], (1, 1)) for part in range(2)]
    total = total[0] + total[1]
    last = [dot(images[part, 2 * R :], images[part, 2 * R :], (1, 1)) for part in range(2)]
    sums[: 2 * R] = total[:, :R]
    sums[2 * R : 4 * R] = total[:, R:]
    sums[4 * R :] = last[0] + last[1]
    z, core = place_ref[0], place_ref[1]
    size = sums_ref.shape[2]
    for d in range(2):
        for k in range(4):
            sums_ref[d, k] = sums[aligned(4 * (core ^ d) + (z ^ k), size)]
    wait(sent)


def finish_kernel(
    place_ref, own_ref, partner_ref, side_ref, basis_0_ref, basis_1_ref, basis_2_ref, solution_ref, residual_ref,
    sums, halves, work, cross, basis, side, solved, left_over, sems,
):
    copies = Copies(sems)
    z, core = place_ref[0], place_ref[1]
    size = own_ref.shape[1]
    for d, ref in enumerate((own_ref, partner_ref)):
        for k in range(4):
            sums[aligned(4 * (core ^ d) + (z ^ k), size)] = ref[k]
    others = [copies.start(side_ref, side)]
    for i, ref in enumerate((basis_0_ref, basis_1_ref, basis_2_ref)):
        others += [copies.start(ref.at[part], basis.at[part, R * i : R * (i + 1)]) for part in range(2)]
    b_0, b_1, a_00, a_10, a_11 = (sums.at[R * i : R * (i + 1)] for i in range(5))
    work[...] = a_00[...]

    def factor(i, carry):
        halves[i] = inverse_factor(work[...])

        @pl.when(i == 0)
        def _():
            cross[...] = dot(halves[0], a_10[...], (1, 1))
            work[...] = a_11[...] - dot(cross[...], cross[...], (0, 0))

        return carry

    lax.fori_loop(0, 2, factor, 0)
    reduced = dot(halves[0], b_0[...])
    tail = dot(halves[1], b_1[...] - dot(cross[...], reduced, (0, 0)))
    y_1 = dot(tail, halves[1], (0, 0))
    y_0 = dot(reduced - dot(cross[...], y_1, (1, 1)), halves[0], (0, 0))
    weights = jnp.concatenate([y_0, y_1], axis=1)
    wait(others)
    sent = []
    for part in range(2):
        solved[part] = dot(weights, basis[part, : 2 * R])
        sent.append(copies.start(solved.at[part], solution_ref.at[part]))
        left_over[part] = side[part] - SHIFT * solved[part] - dot(weights, basis[part, R:])
        sent.append(copies.start(left_over.at[part], residual_ref.at[part]))
    wait(sent)


def swap(x, axis, k):
    n = lax.axis_size(axis)
    return lax.ppermute(x, axis, [(i, i ^ k) for i in range(n)])


def sum_axis(x, axis):
    one, two, three = (swap(x, axis, k) for k in (1, 2, 3))
    return (x + one) + (two + three)


def sum_halves(x):
    total = x[0] + swap(x[1], "c", 1)
    for axis in ("z", "y", "x"):
        total = sum_axis(total, axis)
    return total, swap(total, "c", 1)


def gather_z(piece):
    own = jnp.stack([piece] + [swap(piece, "z", k) for k in (1, 2, 3)])
    return own, swap(own, "c", 1)


def sum_pieces(x):
    pair = x[0] + swap(x[1], "c", 1)
    one, two, three = (swap(pair[k], "z", k) for k in (1, 2, 3))
    total = (pair[0] + one) + (two + three)
    for axis in ("y", "x"):
        total = sum_axis(total, axis)
    return gather_z(total)


def gather_coeffs(products):
    parts = lax.all_to_all(products.reshape(8 * TILES, 16, 2 * K), ALL, 0, 0, tiled=True)
    parts = parts.reshape(TILES, 8, 16, 2 * K)
    return gather_z(jnp.sum(parts.astype(jnp.float32), axis=1).astype(jnp.bfloat16))


def local(right_side, self_impedance, near_blocks, near_columns, column_factors, row_factors, tile_ranks):
    width = right_side.shape[2]
    sub_blocks = near_columns.shape[1]
    x, y, z, core = (lax.axis_index(axis) for axis in ALL)
    place = jnp.stack([z, core]).astype(jnp.int32)
    where = near_columns[0] - (2 * z + core) * sub_blocks + HALO
    ranks = lax.dynamic_index_in_dim(tile_ranks, 4 * x + y, 0, keepdims=False)
    columns = column_factors[0].reshape(TILES * 2 * K, width)
    rows = row_factors[0].reshape(TILES * 2 * K, width)
    near = near_blocks[0]
    forward = [(i, i + 1) for i in range(7)]
    backward = [(i + 1, i) for i in range(7)]

    def shape(*dims, dtype=jnp.float32):
        return jax.ShapeDtypeStruct(dims, dtype)

    block = shape(2, R, width)
    rounded_block = shape(2, R, width, dtype=jnp.bfloat16)
    edge = shape(2, R, HALO * SB, dtype=jnp.bfloat16)
    products_block = shape(TILES, R, 2 * K, dtype=jnp.bfloat16)
    wide = VMEM((2, R, width), jnp.float32)
    rounded_scratch = VMEM((2, R, width), jnp.bfloat16)
    products_scratch = VMEM((TILES, R, 2 * K), jnp.bfloat16)
    weights = VMEM((TILES * 2 * K, width), jnp.bfloat16)
    far_scratch = [products_scratch, VMEM((2 * R, TILES * 2 * K), jnp.bfloat16)]
    square = VMEM((R, R), jnp.float32)
    outer = VMEM((5 * R, R), jnp.float32)
    stacked = VMEM((2, 3 * R, width), jnp.float32)

    def call(kernel, out_specs, smem, vmem, scratch, copies, *args, limit=LARGE):
        if copies:
            scratch = [*scratch, pltpu.SemaphoreType.DMA((copies,))]
        return pl.pallas_call(
            kernel,
            out_shape=tuple(kind for kind, _ in out_specs),
            in_specs=[SMEM] * smem + [WHOLE] * vmem + [ANY] * (len(args) - smem - vmem),
            out_specs=tuple(space for _, space in out_specs),
            scratch_shapes=scratch,
            compiler_params=pltpu.CompilerParams(vmem_limit_bytes=limit),
            cost_estimate=pl.CostEstimate(flops=3 * 10**8, bytes_accessed=6 * 2**20, transcendentals=0),
        )(*args)

    def operate(x, rounded, low, high, products):
        from_right = lax.ppermute(low, ("z", "c"), backward)
        from_left = lax.ppermute(high, ("z", "c"), forward)
        own, partner = gather_coeffs(products)
        (base,) = call(
            near_kernel,
            ((block, ANY),),
            1,
            0,
            [
                wide,
                VMEM((2, R, width + 2 * HALO * SB), jnp.bfloat16),
                VMEM((2, width), jnp.float32),
                VMEM(near.shape, jnp.bfloat16),
                VMEM((2 * R, SLOTS * SB), jnp.bfloat16),
                wide,
            ],
            7,
            where, x, rounded, from_left, from_right, self_impedance, near,
        )
        return own, partner, base

    (gram,) = call(
        gram_kernel, ((shape(2, R // 2, R), WHOLE),), 1, 1, [square], 0, place, right_side, limit=SMALL
    )
    operands = ((block, ANY), (rounded_block, ANY), (edge, ANY), (edge, ANY), (products_block, ANY))
    basis_0, *rest = call(
        start_kernel, operands, 1, 2, [square, wide, weights, wide, rounded_scratch, products_scratch], 10,
        place, *sum_halves(gram), right_side, columns,
    )
    own, partner, base = operate(basis_0, *rest)
    basis_1, *rest = call(
        middle_kernel, operands, 2, 3, [*far_scratch, weights, wide, rounded_scratch, products_scratch], 10,
        place, ranks, own, partner, rows, base, columns,
    )
    own, partner, base = operate(basis_1, *rest)
    basis_2, sums = call(
        last_kernel, ((block, ANY), (shape(2, 4, 5 * R // 8, R), WHOLE)), 2, 3,
        [*far_scratch, VMEM((3, 2, R, width), jnp.float32), stacked, outer], 6,
        place, ranks, own, partner, rows, base, right_side, basis_0, basis_1,
    )
    return call(
        finish_kernel, ((block, ANY), (block, ANY)), 1, 2,
        [outer, VMEM((2, R, R), jnp.float32), square, square, stacked, wide, wide, wide], 11,
        place, *sum_pieces(sums), right_side, basis_0, basis_1, basis_2,
    )


def solution(mesh):
    fine = Mesh(mesh.devices.reshape(4, 4, 4, 2), ALL)
    row, col = ("x", "y"), ("z", "c")
    placed = (
        P(None, None, ALL),
        P(None, ALL),
        P(row, col, None, None, None, None),
        P(row, col, None),
        P(row, None, None, None, col),
        P(row, None, None, None, col),
        P(),
    )
    return jax.shard_map(
        local, mesh=fine, in_specs=placed, out_specs=(P(None, None, ALL), P(None, None, ALL)), check_vma=False
    )
```

profile of v0, /device:TPU:1, one launch (start us, length us, event | category | flops | bytes accessed | tf_op | source)
XLA Modules:
  0.0 190.7 jit_solution(4549787961944784699)
XLA Ops:
  0.7 1.1 copy-done.1
  1.9 1.3 shard_map.86
  3.2 1.5 collective-permute-start
  4.7 0.9 collective-permute-done
  5.6 3.9 %collective-permute-start.3 = (f32[64,128]{1,0:T(8,128)S(1)}, f32[64,128]{1,0:T(8,128)S(1)}, u32[]{:S(2)}, u32[]{:S(2)}) collective-permute-start(f32[64,128]{1,0:T(8,128)S(1)} %fusion.2), channel_id=1, source_target_pairs={{0,6},{2,4},{4,2},{6,0},{1,7},{3,5},{5,3},{7,1},{8,14},{10,12},{12... | collective-permute-start | bytes 98312 | tf_op jit(solution)/shard_map/ppermute | solution.py:306
  9.4 0.7 collective-permute-start.1
  10.7 3.0 %collective-permute-done.2 = f32[64,128]{1,0:T(8,128)S(1)} collective-permute-done((f32[64,128]{1,0:T(8,128)S(1)}, f32[64,128]{1,0:T(8,128)S(1)}, u32[]{:S(2)}, u32[]{:S(2)}) %collective-permute-start.2) | collective-permute-done | bytes 32800 | tf_op jit(solution)/shard_map/ppermute | solution.py:306
  13.7 2.8 %collective-permute-start.6 = (f32[64,128]{1,0:T(8,128)S(1)}, f32[64,128]{1,0:T(8,128)S(1)}, u32[]{:S(2)}, u32[]{:S(2)}) collective-permute-start(f32[64,128]{1,0:T(8,128)S(1)} %add_add_fusion.4), channel_id=1, source_target_pairs={{0,24},{8,16},{16,8},{24,0},{1,25},{9,17},{17,9},{25,1},{2,26},{10... | collective-permute-start | bytes 98312 | tf_op jit(solution)/shard_map/ppermute | solution.py:306
  17.8 3.0 %collective-permute-done.5 = f32[64,128]{1,0:T(8,128)S(1)} collective-permute-done((f32[64,128]{1,0:T(8,128)S(1)}, f32[64,128]{1,0:T(8,128)S(1)}, u32[]{:S(2)}, u32[]{:S(2)}) %collective-permute-start.5) | collective-permute-done | bytes 32800 | tf_op jit(solution)/shard_map/ppermute | solution.py:306
  20.8 2.6 %collective-permute-start.9 = (f32[64,128]{1,0:T(8,128)S(1)}, f32[64,128]{1,0:T(8,128)S(1)}, u32[]{:S(2)}, u32[]{:S(2)}) collective-permute-start(f32[64,128]{1,0:T(8,128)S(1)} %add_add_fusion.3), channel_id=1, source_target_pairs={{0,96},{32,64},{64,32},{96,0},{1,97},{33,65},{65,33},{97,1},{2,98}... | collective-permute-start | bytes 98312 | tf_op jit(solution)/shard_map/ppermute | solution.py:306
  24.2 0.7 collective-permute-done.9
  24.9 2.8 %collective-permute-done.8 = f32[64,128]{1,0:T(8,128)S(1)} collective-permute-done((f32[64,128]{1,0:T(8,128)S(1)}, f32[64,128]{1,0:T(8,128)S(1)}, u32[]{:S(2)}, u32[]{:S(2)}) %collective-permute-start.8) | collective-permute-done | bytes 32800 | tf_op jit(solution)/shard_map/ppermute | solution.py:306
  27.7 4.7 %collective-permute-start.10 = (f32[64,128]{1,0:T(8,128)S(1)}, f32[64,128]{1,0:T(8,128)S(1)}, u32[]{:S(2)}, u32[]{:S(2)}) collective-permute-start(f32[64,128]{1,0:T(8,128)S(1)} %add_add_fusion.2.mine_ref), channel_id=1, source_target_pairs={{0,1},{1,0},{2,3},{3,2},{4,5},{5,4},{6,7},{7,6},{8,9},{9,8},{10,11... | collective-permute-start | bytes 98312 | tf_op jit(solution)/shard_map/ppermute | solution.py:306
  32.4 0.9 collective-permute-done.10.other_ref
  33.9 9.9 %shard_map.87 = (f32[2,128,768]{2,1,0:T(8,128)}, bf16[2,128,768]{2,1,0:T(8,128)(2,1)}, bf16[2,128,256]{2,1,0:T(8,128)(2,1)}, bf16[2,128,256]{2,1,0:T(8,128)(2,1)}, bf16[16,128,128]{2,1,0:T(8,128)(2,1)}) custom-call(s32[2]{0:T(128)} %copy-done.2, f32[64,128]{1,0:T(8,128)} %copy-done.9, f32[64,128]{1,0:T(8,128)} %copy-done.14, f32[2,128,768]{2,1,0:T(8,128)} %side_ref.7, ...), custom_call_target="tpu_custom_call" | custom-call | flops 300000000 | bytes 6291456 | tf_op jit(solution)/shard_map/pallas_call | solution.py:373
  43.7 19.7 %all_to_all.10 = bf16[128,16,128]{2,1,0:T(8,128)(2,1)S(1)} all-to-all(bf16[128,16,128]{2,1,0:T(8,128)(2,1)} %bitcast.56), channel_id=1, replica_groups=mesh['x'=4,'y'=4,'z'=4,'c'=2] {'x','y','z','c'}, dimensions={0} | all-to-all | bytes 1048576 | tf_op jit(solution)/shard_map/all_to_all | solution.py:336
  63.5 0.9 collective-permute-start.13
  64.4 0.7 collective-permute-start.12
  65.1 1.7 collective-permute-start.11
  66.9 3.8 %collective-permute-start.15 = (bf16[2,128,256]{2,1,0:T(8,128)(2,1)}, bf16[2,128,256]{2,1,0:T(8,128)(2,1)S(1)}, u32[]{:S(2)}, u32[]{:S(2)}) collective-permute-start(bf16[2,128,256]{2,1,0:T(8,128)(2,1)} %get-tuple-element.17), channel_id=1, source_target_pairs={{0,1},{1,2},{2,3},{3,4},{4,5},{5,6},{6,7},{8,9},{9,10},{10,11},{11... | collective-permute-start | bytes 393224 | tf_op jit(solution)/shard_map/ppermute | solution.py:385
  70.6 1.9 %collective-permute-start.16 = (bf16[2,128,256]{2,1,0:T(8,128)(2,1)}, bf16[2,128,256]{2,1,0:T(8,128)(2,1)S(1)}, u32[]{:S(2)}, u32[]{:S(2)}) collective-permute-start(bf16[2,128,256]{2,1,0:T(8,128)(2,1)} %get-tuple-element.18), channel_id=1, source_target_pairs={{1,0},{2,1},{3,2},{4,3},{5,4},{6,5},{7,6},{9,8},{10,9},{11,10},{12... | collective-permute-start | bytes 393224 | tf_op jit(solution)/shard_map/ppermute | solution.py:384
  74.0 3.1 %collective-permute-done.16.high_ref = bf16[2,128,256]{2,1,0:T(8,128)(2,1)S(1)} collective-permute-done((bf16[2,128,256]{2,1,0:T(8,128)(2,1)}, bf16[2,128,256]{2,1,0:T(8,128)(2,1)S(1)}, u32[]{:S(2)}, u32[]{:S(2)}) %collective-permute-start.16) | collective-permute-done | bytes 131104 | tf_op jit(solution)/shard_map/ppermute | solution.py:384
  77.1 0.6 copy-done.11
  77.8 6.1 %shard_map.88.base_ref = f32[2,128,768]{2,1,0:T(8,128)} custom-call(s32[6,6]{1,0:T(8,128)} %fusion.4.where_ref, f32[2,128,768]{2,1,0:T(8,128)} %get-tuple-element.15.x_ref.basis_0_ref, bf16[2,128,768]{2,1,0:T(8,128)(2,1)} %get-tuple-element.16.rounded_ref, bf16[2,128,256]{2,1,0:T(8,128)(2,1)} %copy-done.10, bf16[2,128,256]{2,1,0:T(8,128)(2,1)} %copy-done.11, ...), custom_call_target="tpu_custom_call" | custom-call | flops 300000000 | bytes 6291456 | tf_op jit(solution)/shard_map/pallas_call | solution.py:373
  83.9 0.7 copy-done.6
  84.6 7.1 %shard_map.89 = (f32[2,128,768]{2,1,0:T(8,128)}, bf16[2,128,768]{2,1,0:T(8,128)(2,1)}, bf16[2,128,256]{2,1,0:T(8,128)(2,1)}, bf16[2,128,256]{2,1,0:T(8,128)(2,1)}, bf16[16,128,128]{2,1,0:T(8,128)(2,1)}) custom-call(s32[2]{0:T(128)} %copy-done.2, s32[16]{0:T(128)} %dynamic-slice_bitcast_fusion.ranks_ref, bf16[4,16,16,128]{3,2,1,0:T(8,128)(2,1)} %copy-done.3, ...), custom_call_target="tpu_custom_call" | custom-call | flops 300000000 | bytes 6291456 | tf_op jit(solution)/shard_map/pallas_call | solution.py:373
  91.7 17.9 %all_to_all.11 = bf16[128,16,128]{2,1,0:T(8,128)(2,1)S(1)} all-to-all(bf16[128,16,128]{2,1,0:T(8,128)(2,1)} %bitcast.55), channel_id=1, replica_groups=mesh['x'=4,'y'=4,'z'=4,'c'=2] {'x','y','z','c'}, dimensions={0} | all-to-all | bytes 1048576 | tf_op jit(solution)/shard_map/all_to_all | solution.py:336
  109.6 0.9 collective-permute-start.19
  110.5 0.7 collective-permute-start.18
  111.2 1.7 collective-permute-start.17
  112.9 1.1 collective-permute-done.19
  114.0 1.1 collective-permute-done.18
  115.6 2.5 %collective-permute-start.20 = (bf16[4,16,16,128]{3,2,1,0:T(8,128)(2,1)S(1)}, bf16[4,16,16,128]{3,2,1,0:T(8,128)(2,1)S(1)}, u32[]{:S(2)}, u32[]{:S(2)}) collective-permute-start(bf16[4,16,16,128]{3,2,1,0:T(8,128)(2,1)S(1)} %pad_maximum_fusion.1.own_ref), channel_id=1, source_target_pairs={{0,1},{1,0},{2,3},{3,2},{4,5},{5,4},{6,7},{7,6},{8,9},{9,8},{10,11... | collective-permute-start | bytes 786440 | tf_op jit(solution)/shard_map/ppermute | solution.py:306
  118.1 2.9 %collective-permute-start.21 = (bf16[2,128,256]{2,1,0:T(8,128)(2,1)}, bf16[2,128,256]{2,1,0:T(8,128)(2,1)S(1)}, u32[]{:S(2)}, u32[]{:S(2)}) collective-permute-start(bf16[2,128,256]{2,1,0:T(8,128)(2,1)} %get-tuple-element.22), channel_id=1, source_target_pairs={{0,1},{1,2},{2,3},{3,4},{4,5},{5,6},{6,7},{8,9},{9,10},{10,11},{11... | collective-permute-start | bytes 393224 | tf_op jit(solution)/shard_map/ppermute | solution.py:385
  121.0 1.9 %collective-permute-start.22 = (bf16[2,128,256]{2,1,0:T(8,128)(2,1)}, bf16[2,128,256]{2,1,0:T(8,128)(2,1)S(1)}, u32[]{:S(2)}, u32[]{:S(2)}) collective-permute-start(bf16[2,128,256]{2,1,0:T(8,128)(2,1)} %get-tuple-element.23), channel_id=1, source_target_pairs={{1,0},{2,1},{3,2},{4,3},{5,4},{6,5},{7,6},{9,8},{10,9},{11,10},{12... | collective-permute-start | bytes 393224 | tf_op jit(solution)/shard_map/ppermute | solution.py:384
  123.2 4.3 %collective-permute-done.22.high_ref = bf16[2,128,256]{2,1,0:T(8,128)(2,1)S(1)} collective-permute-done((bf16[2,128,256]{2,1,0:T(8,128)(2,1)}, bf16[2,128,256]{2,1,0:T(8,128)(2,1)S(1)}, u32[]{:S(2)}, u32[]{:S(2)}) %collective-permute-start.22) | collective-permute-done | bytes 131104 | tf_op jit(solution)/shard_map/ppermute | solution.py:384
  127.5 0.6 copy-done.13
  128.1 6.1 %shard_map.90.base_ref = f32[2,128,768]{2,1,0:T(8,128)} custom-call(s32[6,6]{1,0:T(8,128)} %fusion.4.where_ref, f32[2,128,768]{2,1,0:T(8,128)} %get-tuple-element.20.x_ref.basis_1_ref, bf16[2,128,768]{2,1,0:T(8,128)(2,1)} %get-tuple-element.21.rounded_ref, bf16[2,128,256]{2,1,0:T(8,128)(2,1)} %copy-done.12, bf16[2,128,256]{2,1,0:T(8,128)(2,1)} %copy-done.13, ...), custom_call_target="tpu_custom_call" | custom-call | flops 300000000 | bytes 6291456 | tf_op jit(solution)/shard_map/pallas_call | solution.py:373
  134.2 0.7 copy-done.7
  134.9 7.7 %shard_map.91 = (f32[2,128,768]{2,1,0:T(8,128)}, f32[2,4,80,128]{3,2,1,0:T(8,128)}) custom-call(s32[2]{0:T(128)} %copy-done.2, s32[16]{0:T(128)} %dynamic-slice_bitcast_fusion.ranks_ref, bf16[4,16,16,128]{3,2,1,0:T(8,128)(2,1)} %copy-done.4, bf16[4,16,16,128]{3,2,1,0:T(8,128)(2,1)} %copy-done.7, bf16[2048,768]{1,0:T(8,128)(2,1)} %bitcast.50, ...), custom_call_target="tpu_custom_call" | custom-call | flops 300000000 | bytes 6291456 | tf_op jit(solution)/shard_map/pallas_call | solution.py:373
  142.7 0.9 slice_bitcast_fusion
  143.7 1.4 collective-permute-done.23
  145.1 0.9 bitcast_add_fusion
  146.5 1.5 collective-permute-start.25
  148.1 1.3 collective-permute-start.24
  149.4 0.8 collective-permute-done.26
  150.2 0.8 collective-permute-done.25
  151.8 1.8 collective-permute-start.28
  153.7 1.2 collective-permute-start.27
  154.8 0.8 collective-permute-done.29
  156.7 0.9 collective-permute-start.32
  157.6 1.2 collective-permute-start.31
  158.9 1.2 collective-permute-start.30
  160.0 0.8 collective-permute-done.32
  160.8 1.2 collective-permute-done.31
  162.0 1.7 collective-permute-start.35
  163.7 0.9 collective-permute-start.34
  164.6 0.7 collective-permute-start.33
  165.3 0.8 collective-permute-done.35
  166.1 2.0 %collective-permute-done.34 = f32[80,128]{1,0:T(8,128)S(1)} collective-permute-done((f32[80,128]{1,0:T(8,128)S(1)}, f32[80,128]{1,0:T(8,128)S(1)}, u32[]{:S(2)}, u32[]{:S(2)}) %collective-permute-start.34) | collective-permute-done | bytes 40992 | tf_op jit(solution)/shard_map/ppermute | solution.py:306
  168.1 6.2 %collective-permute-start.36 = (f32[4,80,128]{2,1,0:T(8,128)S(1)}, f32[4,80,128]{2,1,0:T(8,128)S(1)}, u32[]{:S(2)}, u32[]{:S(2)}) collective-permute-start(f32[4,80,128]{2,1,0:T(8,128)S(1)} %pad_maximum_fusion.2.own_ref), channel_id=1, source_target_pairs={{0,1},{1,0},{2,3},{3,2},{4,5},{5,4},{6,7},{7,6},{8,9},{9,8},{10,11... | collective-permute-start | bytes 491528 | tf_op jit(solution)/shard_map/ppermute | solution.py:306
  174.3 1.0 collective-permute-done.36.partner_ref
  175.3 0.7 copy-done.8
  176.0 14.5 %shard_map.92 = (f32[2,128,768]{2,1,0:T(8,128)}, f32[2,128,768]{2,1,0:T(8,128)}) custom-call(s32[2]{0:T(128)} %copy-done.2, f32[4,80,128]{2,1,0:T(8,128)} %copy-done.5, f32[4,80,128]{2,1,0:T(8,128)} %copy-done.8, f32[2,128,768]{2,1,0:T(8,128)} %side_ref.7, f32[2,128,768]{2,1,0:T(8,128)} %get-tuple-element.15.x_ref.basis_0_ref, ...), custom_call_target="tpu_custom_call" | custom-call | flops 300000000 | bytes 6291456 | tf_op jit(solution)/shard_map/pallas_call | solution.py:373
  (70 shorter events, 8.3 us)
Async XLA Ops:
  0.6 72.9 %copy-start = (s32[16,16]{1,0:T(8,128)S(1)}, s32[16,16]{1,0:T(8,128)}, u32[]{:S(2)}) copy-start(s32[16,16]{1,0:T(8,128)} %param.13) | copy-start | bytes 3076
  0.7 1.1 copy-start.1
  1.9 31.4 %copy-start.2 = (s32[2]{0:T(128)}, s32[2]{0:T(128)S(1)}, u32[]{:S(2)}) copy-start(s32[2]{0:T(128)S(1)} %pad_add_fusion.place_ref) | copy-start | bytes 28
  3.2 2.3 %collective-permute-start = (f32[64,128]{1,0:T(8,128)S(1)}, f32[64,128]{1,0:T(8,128)S(1)}, u32[]{:S(2)}, u32[]{:S(2)}) collective-permute-start(f32[64,128]{1,0:T(8,128)S(1)} %slice_bitcast_fusion.5), channel_id=1, source_target_pairs={{0,1},{1,0},{2,3},{3,2},{4,5},{5,4},{6,7},{7,6},{8,9},{9,8},{10,11... | collective-permute-start | bytes 98312 | tf_op jit(solution)/shard_map/ppermute | solution.py:306
  5.6 5.2 %collective-permute-start.3 = (f32[64,128]{1,0:T(8,128)S(1)}, f32[64,128]{1,0:T(8,128)S(1)}, u32[]{:S(2)}, u32[]{:S(2)}) collective-permute-start(f32[64,128]{1,0:T(8,128)S(1)} %fusion.2), channel_id=1, source_target_pairs={{0,6},{2,4},{4,2},{6,0},{1,7},{3,5},{5,3},{7,1},{8,14},{10,12},{12... | collective-permute-start | bytes 98312 | tf_op jit(solution)/shard_map/ppermute | solution.py:306
  9.4 4.3 %collective-permute-start.2 = (f32[64,128]{1,0:T(8,128)S(1)}, f32[64,128]{1,0:T(8,128)S(1)}, u32[]{:S(2)}, u32[]{:S(2)}) collective-permute-start(f32[64,128]{1,0:T(8,128)S(1)} %fusion.2), channel_id=1, source_target_pairs={{0,4},{2,6},{4,0},{6,2},{1,5},{3,7},{5,1},{7,3},{8,12},{10,14},{12... | collective-permute-start | bytes 98312 | tf_op jit(solution)/shard_map/ppermute | solution.py:306
  9.4 4.3 %collective-permute-start.1 = (f32[64,128]{1,0:T(8,128)S(1)}, f32[64,128]{1,0:T(8,128)S(1)}, u32[]{:S(2)}, u32[]{:S(2)}) collective-permute-start(f32[64,128]{1,0:T(8,128)S(1)} %fusion.2), channel_id=1, source_target_pairs={{0,2},{2,0},{4,6},{6,4},{1,3},{3,1},{5,7},{7,5},{8,10},{10,8},{12,... | collective-permute-start | bytes 98312 | tf_op jit(solution)/shard_map/ppermute | solution.py:306
  13.7 4.1 %collective-permute-start.6 = (f32[64,128]{1,0:T(8,128)S(1)}, f32[64,128]{1,0:T(8,128)S(1)}, u32[]{:S(2)}, u32[]{:S(2)}) collective-permute-start(f32[64,128]{1,0:T(8,128)S(1)} %add_add_fusion.4), channel_id=1, source_target_pairs={{0,24},{8,16},{16,8},{24,0},{1,25},{9,17},{17,9},{25,1},{2,26},{10... | collective-permute-start | bytes 98312 | tf_op jit(solution)/shard_map/ppermute | solution.py:306
  16.5 4.3 %collective-permute-start.5 = (f32[64,128]{1,0:T(8,128)S(1)}, f32[64,128]{1,0:T(8,128)S(1)}, u32[]{:S(2)}, u32[]{:S(2)}) collective-permute-start(f32[64,128]{1,0:T(8,128)S(1)} %add_add_fusion.4), channel_id=1, source_target_pairs={{0,16},{8,24},{16,0},{24,8},{1,17},{9,25},{17,1},{25,9},{2,18},{10... | collective-permute-start | bytes 98312 | tf_op jit(solution)/shard_map/ppermute | solution.py:306
  16.9 3.9 %collective-permute-start.4 = (f32[64,128]{1,0:T(8,128)S(1)}, f32[64,128]{1,0:T(8,128)S(1)}, u32[]{:S(2)}, u32[]{:S(2)}) collective-permute-start(f32[64,128]{1,0:T(8,128)S(1)} %add_add_fusion.4), channel_id=1, source_target_pairs={{0,8},{8,0},{16,24},{24,16},{1,9},{9,1},{17,25},{25,17},{2,10},{10... | collective-permute-start | bytes 98312 | tf_op jit(solution)/shard_map/ppermute | solution.py:306
  20.8 52.1 %copy-start.15 = (s32[1,6,6]{2,0,1:T(1,128)S(1)}, s32[1,6,6]{2,0,1:T(1,128)}, u32[]{:S(2)}) copy-start(s32[1,6,6]{2,0,1:T(1,128)} %param.10) | copy-start | bytes 436
  20.8 4.1 %collective-permute-start.9 = (f32[64,128]{1,0:T(8,128)S(1)}, f32[64,128]{1,0:T(8,128)S(1)}, u32[]{:S(2)}, u32[]{:S(2)}) collective-permute-start(f32[64,128]{1,0:T(8,128)S(1)} %add_add_fusion.3), channel_id=1, source_target_pairs={{0,96},{32,64},{64,32},{96,0},{1,97},{33,65},{65,33},{97,1},{2,98}... | collective-permute-start | bytes 98312 | tf_op jit(solution)/shard_map/ppermute | solution.py:306
  23.4 4.3 %collective-permute-start.8 = (f32[64,128]{1,0:T(8,128)S(1)}, f32[64,128]{1,0:T(8,128)S(1)}, u32[]{:S(2)}, u32[]{:S(2)}) collective-permute-start(f32[64,128]{1,0:T(8,128)S(1)} %add_add_fusion.3), channel_id=1, source_target_pairs={{0,64},{32,96},{64,0},{96,32},{1,65},{33,97},{65,1},{97,33},{2,66}... | collective-permute-start | bytes 98312 | tf_op jit(solution)/shard_map/ppermute | solution.py:306
  23.9 3.7 %collective-permute-start.7 = (f32[64,128]{1,0:T(8,128)S(1)}, f32[64,128]{1,0:T(8,128)S(1)}, u32[]{:S(2)}, u32[]{:S(2)}) collective-permute-start(f32[64,128]{1,0:T(8,128)S(1)} %add_add_fusion.3), channel_id=1, source_target_pairs={{0,32},{32,0},{64,96},{96,64},{1,33},{33,1},{65,97},{97,65},{2,34}... | collective-permute-start | bytes 98312 | tf_op jit(solution)/shard_map/ppermute | solution.py:306
  27.7 5.6 %copy-start.9 = (f32[64,128]{1,0:T(8,128)}, f32[64,128]{1,0:T(8,128)S(1)}, u32[]{:S(2)}) copy-start(f32[64,128]{1,0:T(8,128)S(1)} %add_add_fusion.2.mine_ref) | copy-start | bytes 98308
  27.7 5.6 %collective-permute-start.10 = (f32[64,128]{1,0:T(8,128)S(1)}, f32[64,128]{1,0:T(8,128)S(1)}, u32[]{:S(2)}, u32[]{:S(2)}) collective-permute-start(f32[64,128]{1,0:T(8,128)S(1)} %add_add_fusion.2.mine_ref), channel_id=1, source_target_pairs={{0,1},{1,0},{2,3},{3,2},{4,5},{5,4},{6,7},{7,6},{8,9},{9,8},{10,11... | collective-permute-start | bytes 98312 | tf_op jit(solution)/shard_map/ppermute | solution.py:306
  33.3 0.6 copy-start.14
  63.5 9.0 %collective-permute-start.13 = (bf16[16,16,128]{2,1,0:T(8,128)(2,1)S(1)}, bf16[16,16,128]{2,1,0:T(8,128)(2,1)S(1)}, u32[]{:S(2)}, u32[]{:S(2)}) collective-permute-start(bf16[16,16,128]{2,1,0:T(8,128)(2,1)S(1)} %bitcast_reduce_fusion.1), channel_id=1, source_target_pairs={{0,6},{2,4},{4,2},{6,0},{1,7},{3,5},{5,3},{7,1},{8,14},{10,12},{12... | collective-permute-start | bytes 196616 | tf_op jit(solution)/shard_map/ppermute | solution.py:306
  64.4 8.1 %collective-permute-start.12 = (bf16[16,16,128]{2,1,0:T(8,128)(2,1)S(1)}, bf16[16,16,128]{2,1,0:T(8,128)(2,1)S(1)}, u32[]{:S(2)}, u32[]{:S(2)}) collective-permute-start(bf16[16,16,128]{2,1,0:T(8,128)(2,1)S(1)} %bitcast_reduce_fusion.1), channel_id=1, source_target_pairs={{0,4},{2,6},{4,0},{6,2},{1,5},{3,7},{5,1},{7,3},{8,12},{10,14},{12... | collective-permute-start | bytes 196616 | tf_op jit(solution)/shard_map/ppermute | solution.py:306
  65.1 7.5 %collective-permute-start.11 = (bf16[16,16,128]{2,1,0:T(8,128)(2,1)S(1)}, bf16[16,16,128]{2,1,0:T(8,128)(2,1)S(1)}, u32[]{:S(2)}, u32[]{:S(2)}) collective-permute-start(bf16[16,16,128]{2,1,0:T(8,128)(2,1)S(1)} %bitcast_reduce_fusion.1), channel_id=1, source_target_pairs={{0,2},{2,0},{4,6},{6,4},{1,3},{3,1},{5,7},{7,5},{8,10},{10,8},{12,... | collective-permute-start | bytes 196616 | tf_op jit(solution)/shard_map/ppermute | solution.py:306
  66.9 7.2 %collective-permute-start.15 = (bf16[2,128,256]{2,1,0:T(8,128)(2,1)}, bf16[2,128,256]{2,1,0:T(8,128)(2,1)S(1)}, u32[]{:S(2)}, u32[]{:S(2)}) collective-permute-start(bf16[2,128,256]{2,1,0:T(8,128)(2,1)} %get-tuple-element.17), channel_id=1, source_target_pairs={{0,1},{1,2},{2,3},{3,4},{4,5},{5,6},{6,7},{8,9},{9,10},{10,11},{11... | collective-permute-start | bytes 393224 | tf_op jit(solution)/shard_map/ppermute | solution.py:385
  70.6 6.5 %collective-permute-start.16 = (bf16[2,128,256]{2,1,0:T(8,128)(2,1)}, bf16[2,128,256]{2,1,0:T(8,128)(2,1)S(1)}, u32[]{:S(2)}, u32[]{:S(2)}) collective-permute-start(bf16[2,128,256]{2,1,0:T(8,128)(2,1)} %get-tuple-element.18), channel_id=1, source_target_pairs={{1,0},{2,1},{3,2},{4,3},{5,4},{6,5},{7,6},{9,8},{10,9},{11,10},{12... | collective-permute-start | bytes 393224 | tf_op jit(solution)/shard_map/ppermute | solution.py:384
  72.6 11.2 %copy-start.3 = (bf16[4,16,16,128]{3,2,1,0:T(8,128)(2,1)}, bf16[4,16,16,128]{3,2,1,0:T(8,128)(2,1)S(1)}, u32[]{:S(2)}) copy-start(bf16[4,16,16,128]{3,2,1,0:T(8,128)(2,1)S(1)} %pad_maximum_fusion.own_ref) | copy-start | bytes 786436
  72.7 11.2 %collective-permute-start.14 = (bf16[4,16,16,128]{3,2,1,0:T(8,128)(2,1)S(1)}, bf16[4,16,16,128]{3,2,1,0:T(8,128)(2,1)S(1)}, u32[]{:S(2)}, u32[]{:S(2)}) collective-permute-start(bf16[4,16,16,128]{3,2,1,0:T(8,128)(2,1)S(1)} %pad_maximum_fusion.own_ref), channel_id=1, source_target_pairs={{0,1},{1,0},{2,3},{3,2},{4,5},{5,4},{6,7},{7,6},{8,9},{9,8},{10,11... | collective-permute-start | bytes 786440 | tf_op jit(solution)/shard_map/ppermute | solution.py:306
  74.0 3.1 %copy-start.10 = (bf16[2,128,256]{2,1,0:T(8,128)(2,1)}, bf16[2,128,256]{2,1,0:T(8,128)(2,1)S(1)}, u32[]{:S(2)}) copy-start(bf16[2,128,256]{2,1,0:T(8,128)(2,1)S(1)} %collective-permute-done.15.low_ref) | copy-start | bytes 393220
  77.1 0.6 copy-start.11
  83.9 0.7 copy-start.6
  109.6 4.4 %collective-permute-start.19 = (bf16[16,16,128]{2,1,0:T(8,128)(2,1)S(1)}, bf16[16,16,128]{2,1,0:T(8,128)(2,1)S(1)}, u32[]{:S(2)}, u32[]{:S(2)}) collective-permute-start(bf16[16,16,128]{2,1,0:T(8,128)(2,1)S(1)} %bitcast_reduce_fusion), channel_id=1, source_target_pairs={{0,6},{2,4},{4,2},{6,0},{1,7},{3,5},{5,3},{7,1},{8,14},{10,12},{12... | collective-permute-start | bytes 196616 | tf_op jit(solution)/shard_map/ppermute | solution.py:306
  110.5 4.6 %collective-permute-start.18 = (bf16[16,16,128]{2,1,0:T(8,128)(2,1)S(1)}, bf16[16,16,128]{2,1,0:T(8,128)(2,1)S(1)}, u32[]{:S(2)}, u32[]{:S(2)}) collective-permute-start(bf16[16,16,128]{2,1,0:T(8,128)(2,1)S(1)} %bitcast_reduce_fusion), channel_id=1, source_target_pairs={{0,4},{2,6},{4,0},{6,2},{1,5},{3,7},{5,1},{7,3},{8,12},{10,14},{12... | collective-permute-start | bytes 196616 | tf_op jit(solution)/shard_map/ppermute | solution.py:306
  111.2 4.4 %collective-permute-start.17 = (bf16[16,16,128]{2,1,0:T(8,128)(2,1)S(1)}, bf16[16,16,128]{2,1,0:T(8,128)(2,1)S(1)}, u32[]{:S(2)}, u32[]{:S(2)}) collective-permute-start(bf16[16,16,128]{2,1,0:T(8,128)(2,1)S(1)} %bitcast_reduce_fusion), channel_id=1, source_target_pairs={{0,2},{2,0},{4,6},{6,4},{1,3},{3,1},{5,7},{7,5},{8,10},{10,8},{12,... | collective-permute-start | bytes 196616 | tf_op jit(solution)/shard_map/ppermute | solution.py:306
  115.6 18.6 %copy-start.4 = (bf16[4,16,16,128]{3,2,1,0:T(8,128)(2,1)}, bf16[4,16,16,128]{3,2,1,0:T(8,128)(2,1)S(1)}, u32[]{:S(2)}) copy-start(bf16[4,16,16,128]{3,2,1,0:T(8,128)(2,1)S(1)} %pad_maximum_fusion.1.own_ref) | copy-start | bytes 786436
  115.6 18.6 %collective-permute-start.20 = (bf16[4,16,16,128]{3,2,1,0:T(8,128)(2,1)S(1)}, bf16[4,16,16,128]{3,2,1,0:T(8,128)(2,1)S(1)}, u32[]{:S(2)}, u32[]{:S(2)}) collective-permute-start(bf16[4,16,16,128]{3,2,1,0:T(8,128)(2,1)S(1)} %pad_maximum_fusion.1.own_ref), channel_id=1, source_target_pairs={{0,1},{1,0},{2,3},{3,2},{4,5},{5,4},{6,7},{7,6},{8,9},{9,8},{10,11... | collective-permute-start | bytes 786440 | tf_op jit(solution)/shard_map/ppermute | solution.py:306
  118.1 5.1 %collective-permute-start.21 = (bf16[2,128,256]{2,1,0:T(8,128)(2,1)}, bf16[2,128,256]{2,1,0:T(8,128)(2,1)S(1)}, u32[]{:S(2)}, u32[]{:S(2)}) collective-permute-start(bf16[2,128,256]{2,1,0:T(8,128)(2,1)} %get-tuple-element.22), channel_id=1, source_target_pairs={{0,1},{1,2},{2,3},{3,4},{4,5},{5,6},{6,7},{8,9},{9,10},{10,11},{11... | collective-permute-start | bytes 393224 | tf_op jit(solution)/shard_map/ppermute | solution.py:385
  121.0 6.5 %collective-permute-start.22 = (bf16[2,128,256]{2,1,0:T(8,128)(2,1)}, bf16[2,128,256]{2,1,0:T(8,128)(2,1)S(1)}, u32[]{:S(2)}, u32[]{:S(2)}) collective-permute-start(bf16[2,128,256]{2,1,0:T(8,128)(2,1)} %get-tuple-element.23), channel_id=1, source_target_pairs={{1,0},{2,1},{3,2},{4,3},{5,4},{6,5},{7,6},{9,8},{10,9},{11,10},{12... | collective-permute-start | bytes 393224 | tf_op jit(solution)/shard_map/ppermute | solution.py:384
  123.2 4.3 %copy-start.12 = (bf16[2,128,256]{2,1,0:T(8,128)(2,1)}, bf16[2,128,256]{2,1,0:T(8,128)(2,1)S(1)}, u32[]{:S(2)}) copy-start(bf16[2,128,256]{2,1,0:T(8,128)(2,1)S(1)} %collective-permute-done.21.low_ref) | copy-start | bytes 393220
  127.5 0.7 copy-start.13
  134.2 0.7 copy-start.7
  143.6 1.5 collective-permute-start.23
  146.0 4.1 %collective-permute-start.26 = (f32[80,128]{1,0:T(8,128)S(1)}, f32[80,128]{1,0:T(8,128)S(1)}, u32[]{:S(2)}, u32[]{:S(2)}) collective-permute-start(f32[80,128]{1,0:T(8,128)S(1)} %get-tuple-element.26), channel_id=1, source_target_pairs={{0,6},{2,4},{4,2},{6,0},{1,7},{3,5},{5,3},{7,1},{8,14},{10,12},{12... | collective-permute-start | bytes 122888 | tf_op jit(solution)/shard_map/ppermute | solution.py:306
  146.5 4.5 %collective-permute-start.25 = (f32[80,128]{1,0:T(8,128)S(1)}, f32[80,128]{1,0:T(8,128)S(1)}, u32[]{:S(2)}, u32[]{:S(2)}) collective-permute-start(f32[80,128]{1,0:T(8,128)S(1)} %get-tuple-element.27), channel_id=1, source_target_pairs={{0,4},{2,6},{4,0},{6,2},{1,5},{3,7},{5,1},{7,3},{8,12},{10,14},{12... | collective-permute-start | bytes 122888 | tf_op jit(solution)/shard_map/ppermute | solution.py:306
  148.1 3.4 %collective-permute-start.24 = (f32[80,128]{1,0:T(8,128)S(1)}, f32[80,128]{1,0:T(8,128)S(1)}, u32[]{:S(2)}, u32[]{:S(2)}) collective-permute-start(f32[80,128]{1,0:T(8,128)S(1)} %get-tuple-element.28), channel_id=1, source_target_pairs={{0,2},{2,0},{4,6},{6,4},{1,3},{3,1},{5,7},{7,5},{8,10},{10,8},{12,... | collective-permute-start | bytes 122888 | tf_op jit(solution)/shard_map/ppermute | solution.py:306
  151.5 4.1 %collective-permute-start.29 = (f32[80,128]{1,0:T(8,128)S(1)}, f32[80,128]{1,0:T(8,128)S(1)}, u32[]{:S(2)}, u32[]{:S(2)}) collective-permute-start(f32[80,128]{1,0:T(8,128)S(1)} %fusion.1), channel_id=1, source_target_pairs={{0,24},{8,16},{16,8},{24,0},{1,25},{9,17},{17,9},{25,1},{2,26},{10... | collective-permute-start | bytes 122888 | tf_op jit(solution)/shard_map/ppermute | solution.py:306
  151.8 4.4 %collective-permute-start.28 = (f32[80,128]{1,0:T(8,128)S(1)}, f32[80,128]{1,0:T(8,128)S(1)}, u32[]{:S(2)}, u32[]{:S(2)}) collective-permute-start(f32[80,128]{1,0:T(8,128)S(1)} %fusion.1), channel_id=1, source_target_pairs={{0,16},{8,24},{16,0},{24,8},{1,17},{9,25},{17,1},{25,9},{2,18},{10... | collective-permute-start | bytes 122888 | tf_op jit(solution)/shard_map/ppermute | solution.py:306
  153.7 3.0 %collective-permute-start.27 = (f32[80,128]{1,0:T(8,128)S(1)}, f32[80,128]{1,0:T(8,128)S(1)}, u32[]{:S(2)}, u32[]{:S(2)}) collective-permute-start(f32[80,128]{1,0:T(8,128)S(1)} %fusion.1), channel_id=1, source_target_pairs={{0,8},{8,0},{16,24},{24,16},{1,9},{9,1},{17,25},{25,17},{2,10},{10... | collective-permute-start | bytes 122888 | tf_op jit(solution)/shard_map/ppermute | solution.py:306
  156.7 4.1 %collective-permute-start.32 = (f32[80,128]{1,0:T(8,128)S(1)}, f32[80,128]{1,0:T(8,128)S(1)}, u32[]{:S(2)}, u32[]{:S(2)}) collective-permute-start(f32[80,128]{1,0:T(8,128)S(1)} %add_add_fusion.1), channel_id=1, source_target_pairs={{0,96},{32,64},{64,32},{96,0},{1,97},{33,65},{65,33},{97,1},{2,98}... | collective-permute-start | bytes 122888 | tf_op jit(solution)/shard_map/ppermute | solution.py:306
  157.6 4.4 %collective-permute-start.31 = (f32[80,128]{1,0:T(8,128)S(1)}, f32[80,128]{1,0:T(8,128)S(1)}, u32[]{:S(2)}, u32[]{:S(2)}) collective-permute-start(f32[80,128]{1,0:T(8,128)S(1)} %add_add_fusion.1), channel_id=1, source_target_pairs={{0,64},{32,96},{64,0},{96,32},{1,65},{33,97},{65,1},{97,33},{2,66}... | collective-permute-start | bytes 122888 | tf_op jit(solution)/shard_map/ppermute | solution.py:306
  158.9 3.1 %collective-permute-start.30 = (f32[80,128]{1,0:T(8,128)S(1)}, f32[80,128]{1,0:T(8,128)S(1)}, u32[]{:S(2)}, u32[]{:S(2)}) collective-permute-start(f32[80,128]{1,0:T(8,128)S(1)} %add_add_fusion.1), channel_id=1, source_target_pairs={{0,32},{32,0},{64,96},{96,64},{1,33},{33,1},{65,97},{97,65},{2,34}... | collective-permute-start | bytes 122888 | tf_op jit(solution)/shard_map/ppermute | solution.py:306
  162.0 4.1 %collective-permute-start.35 = (f32[80,128]{1,0:T(8,128)S(1)}, f32[80,128]{1,0:T(8,128)S(1)}, u32[]{:S(2)}, u32[]{:S(2)}) collective-permute-start(f32[80,128]{1,0:T(8,128)S(1)} %add_add_fusion), channel_id=1, source_target_pairs={{0,6},{2,4},{4,2},{6,0},{1,7},{3,5},{5,3},{7,1},{8,14},{10,12},{12... | collective-permute-start | bytes 122888 | tf_op jit(solution)/shard_map/ppermute | solution.py:306
  163.7 4.4 %collective-permute-start.34 = (f32[80,128]{1,0:T(8,128)S(1)}, f32[80,128]{1,0:T(8,128)S(1)}, u32[]{:S(2)}, u32[]{:S(2)}) collective-permute-start(f32[80,128]{1,0:T(8,128)S(1)} %add_add_fusion), channel_id=1, source_target_pairs={{0,4},{2,6},{4,0},{6,2},{1,5},{3,7},{5,1},{7,3},{8,12},{10,14},{12... | collective-permute-start | bytes 122888 | tf_op jit(solution)/shard_map/ppermute | solution.py:306
  164.6 3.5 %collective-permute-start.33 = (f32[80,128]{1,0:T(8,128)S(1)}, f32[80,128]{1,0:T(8,128)S(1)}, u32[]{:S(2)}, u32[]{:S(2)}) collective-permute-start(f32[80,128]{1,0:T(8,128)S(1)} %add_add_fusion), channel_id=1, source_target_pairs={{0,2},{2,0},{4,6},{6,4},{1,3},{3,1},{5,7},{7,5},{8,10},{10,8},{12,... | collective-permute-start | bytes 122888 | tf_op jit(solution)/shard_map/ppermute | solution.py:306
  168.1 7.2 %copy-start.5 = (f32[4,80,128]{2,1,0:T(8,128)}, f32[4,80,128]{2,1,0:T(8,128)S(1)}, u32[]{:S(2)}) copy-start(f32[4,80,128]{2,1,0:T(8,128)S(1)} %pad_maximum_fusion.2.own_ref) | copy-start | bytes 491524
  168.1 7.2 %collective-permute-start.36 = (f32[4,80,128]{2,1,0:T(8,128)S(1)}, f32[4,80,128]{2,1,0:T(8,128)S(1)}, u32[]{:S(2)}, u32[]{:S(2)}) collective-permute-start(f32[4,80,128]{2,1,0:T(8,128)S(1)} %pad_maximum_fusion.2.own_ref), channel_id=1, source_target_pairs={{0,1},{1,0},{2,3},{3,2},{4,5},{5,4},{6,7},{7,6},{8,9},{9,8},{10,11... | collective-permute-start | bytes 491528 | tf_op jit(solution)/shard_map/ppermute | solution.py:306
  175.3 0.7 copy-start.8
where the time goes:
time: 191 us
  starting transfers between devices  57 us (30%)
  Pallas kernels  52.7 us (28%)
  blocking collectives  37.6 us (20%)
  waiting for transfers between devices  33.8 us (18%)
  local copies, waits for them, and re-layouts  6.56 us (3%)
    pallas_call x7, Pallas kernels, call(): pl.pallas_call(kernel, out_shape=tuple((kind for kind, _ in out_specs)),...  52.7 us
    ppermute x33, starting transfers between devices, swap(): return lax.ppermute(x, axis, [(i, i ^ k) for i in range(n)])  46.5 us
    all_to_all x2, blocking collectives, gather_coeffs(): lax.all_to_all(products.reshape(8 * TILES, 16, 2 * K), ALL, 0, 0, tiled=T...  37.6 us
    ppermute x33, waiting for transfers between devices, swap(): return lax.ppermute(x, axis, [(i, i ^ k) for i in range(n)])  26.2 us
    ppermute x2, waiting for transfers between devices, operate(): from_right = lax.ppermute(low, ('z', 'c'), backward)  7.36 us
    ppermute x2, starting transfers between devices, operate(): from_left = lax.ppermute(high, ('z', 'c'), forward)  6.63 us
    unnamed x32, local copies, waits for them, and re-layouts  5.13 us
    ppermute x2, starting transfers between devices, operate(): from_right = lax.ppermute(low, ('z', 'c'), backward)  3.84 us
  transfers between devices with their start and end apart: 37, of which 26 were waited for; matrix products, arithmetic and copies ran while one was open for 1% of the time, Pallas kernels for 6%

commit v1 on v0

--- a/solution.py
+++ b/solution.py
@@ -20,7 +20,7 @@
 SMEM = pl.BlockSpec(memory_space=pltpu.SMEM)
 ANY = pl.BlockSpec(memory_space=pl.ANY)
 WHOLE = pl.BlockSpec(memory_space=pltpu.VMEM)
-SMALL, LARGE = 12 * 2**20, 60 * 1024 * 1024
+SMALL, LARGE = 12 * 2**20, 60 * 2**20
 
 
 def dot(a, b, over=(1, 0), precision=TOP):
@@ -54,17 +54,35 @@
         rows = [jnp.where(inside, jnp.where(lane == start + t, 1.0, 0.0), rows[t]) for t in range(8)]
         inverse = [None] * 8
         unit = [[None] * 8 for _ in range(8)]
-        for t in range(8):
-            pivots[t][t] = jnp.maximum(pivots[t][t], least[t])
-            inverse[t] = 1.0 / pivots[t][t]
-            for u in range(t + 1, 8):
-                factor = pivots[t][u] * inverse[t]
-                rows[u] = rows[u] - factor * rows[t]
-                for s in range(t):
-                    unit[u][s] = unit[u][s] - factor * unit[t][s]
-                unit[u][t] = -factor
+
+        def eliminate(u, t, factor):
+            rows[u] = rows[u] - factor * rows[t]
+            for s in range(t):
+                unit[u][s] = unit[u][s] - factor * unit[t][s] if s in known[u] else -factor * unit[t][s]
+                known[u].add(s)
+            unit[u][t] = -factor
+            known[u].add(t)
+
+        known = [set() for _ in range(8)]
+        for t in range(0, 8, 2):
+            n = t + 1
+            first = jnp.maximum(pivots[t][t], least[t])
+            off, second = pivots[t][n], pivots[n][n]
+            area = jnp.maximum(first * second - off * off, first * least[n])
+            by_first, by_area = 1.0 / first, 1.0 / area
+            pivots[t][t], inverse[t] = first, by_first
+            pivots[n][n], inverse[n] = area * by_first, first * by_area
+            ratio = off * by_first
+            left = {u: (second * pivots[t][u] - off * pivots[n][u]) * by_area for u in range(t + 2, 8)}
+            right = {u: (first * pivots[n][u] - off * pivots[t][u]) * by_area for u in range(t + 2, 8)}
+            plain = {u: pivots[t][u] * by_first for u in range(t + 2, 8)}
+            for u in range(t + 2, 8):
                 for v in range(u, 8):
-                    pivots[u][v] = pivots[u][v] - factor * pivots[t][v]
+                    pivots[u][v] = pivots[u][v] - (left[u] * pivots[t][v] + right[u] * pivots[n][v])
+            eliminate(n, t, ratio)
+            for u in range(t + 2, 8):
+                eliminate(u, t, plain[u])
+                eliminate(u, n, right[u])
         done = jnp.zeros((8, R), jnp.float32)
         for t in range(8):
             done = jnp.where(sub == t, rows[t] * lax.rsqrt(pivots[t][t]), done)
@@ -108,11 +126,13 @@
     flat = x.reshape(2 * R, x.shape[2])
     sign = jnp.where(lax.broadcasted_iota(jnp.int32, (R, 2 * K), 1) < K, -1.0, 1.0)
     sent = []
-    for i in range(TILES):
-        both = bf16_dot(flat, columns[2 * K * i : 2 * K * (i + 1)], (1, 1))
-        out[i] = (both[:R] + sign * pltpu.roll(both[R:], K, 1)).astype(jnp.bfloat16)
-        if i % 4 == 3:
-            sent.append(copies.start(out.at[i - 3 : i + 1], out_ref.at[i - 3 : i + 1]))
+    for i in range(0, TILES, 2):
+        both = bf16_dot(flat, columns[2 * K * i : 2 * K * (i + 2)], (1, 1))
+        for j in range(2):
+            top, bottom = (both[R * h : R * (h + 1), R * j : R * (j + 1)] for h in range(2))
+            out[i + j] = (top + sign * pltpu.roll(bottom, K, 1)).astype(jnp.bfloat16)
+        if i % 4 == 2:
+            sent.append(copies.start(out.at[i - 2 : i + 2], out_ref.at[i - 2 : i + 2]))
     return sent
 
 
@@ -126,11 +146,11 @@
     ]
 
 
-def gram_kernel(place_ref, side_ref, out_ref, whole):
+def gram_kernel(place_ref, side_ref, mine_ref, other_ref, whole):
     whole[...] = dot(side_ref[0], side_ref[0], (1, 1)) + dot(side_ref[1], side_ref[1], (1, 1))
     core = place_ref[1]
-    for d in range(2):
-        out_ref[d] = whole[aligned(core ^ d, R // 2)]
+    for d, ref in enumerate((mine_ref, other_ref)):
+        ref[...] = whole[aligned(core ^ d, R // 2)]
 
 
 def start_kernel(
@@ -199,28 +219,30 @@
         tiles[:, aligned(chunk + 1 - core, 16)] = partner_ref[k]
 
 
-def far_part(place_ref, ranks_ref, own_ref, partner_ref, rows, tiles, left):
+def far_part(place_ref, ranks_ref, own_ref, partner_ref, rows_copy, rows, tiles, left):
     place_tiles(place_ref, own_ref, partner_ref, tiles)
     lane = lax.broadcasted_iota(jnp.int32, (R, 2 * K), 1)
     rank = jnp.where(lane < K, lane, lane - K)
     sign = jnp.where(lane < K, 1.0, -1.0)
     for j in range(TILES):
-        tile = jnp.where(rank < ranks_ref[j], tiles[j].astype(jnp.float32), 0.0)
+        tile = jnp.where(rank < ranks_ref[place_ref[2], j], tiles[j].astype(jnp.float32), 0.0)
         at = slice(2 * K * j, 2 * K * (j + 1))
         left[:R, at] = (tile * sign).astype(jnp.bfloat16)
         left[R:, at] = pltpu.roll(tile, K, 1).astype(jnp.bfloat16)
+    rows_copy.wait()
     return bf16_dot(left[...], rows[...]).reshape(2, R, rows.shape[1])
 
 
 def middle_kernel(
-    place_ref, ranks_ref, own_ref, partner_ref, rows, base_ref, columns_ref,
+    place_ref, ranks_ref, own_ref, partner_ref, rows_ref, base_ref, columns_ref,
     basis_ref, rounded_ref, low_ref, high_ref, out_ref,
-    tiles, left, columns, basis, rounded, out, sems,
+    tiles, left, rows, columns, basis, rounded, out, sems,
 ):
     copies = Copies(sems)
+    rows_copy = copies.start(rows_ref, rows)
     base_copy = copies.start(base_ref, basis)
     columns_copy = copies.start(columns_ref, columns)
-    far = far_part(place_ref, ranks_ref, own_ref, partner_ref, rows, tiles, left)
+    far = far_part(place_ref, ranks_ref, own_ref, partner_ref, rows_copy, rows, tiles, left)
     base_copy.wait()
     basis[...] = basis[...] + far
     x = basis[...].astype(jnp.bfloat16)
@@ -232,13 +254,14 @@
 
 
 def last_kernel(
-    place_ref, ranks_ref, own_ref, partner_ref, rows, base_ref, side_ref, basis_0_ref, basis_1_ref,
-    basis_2_ref, sums_ref, tiles, left, basis, images, sums, sems,
+    place_ref, ranks_ref, own_ref, partner_ref, rows_ref, base_ref, side_ref, basis_0_ref, basis_1_ref,
+    basis_2_ref, mine_ref, other_ref, tiles, left, rows, basis, images, sums, sems,
 ):
     copies = Copies(sems)
+    rows_copy = copies.start(rows_ref, rows)
     others = [copies.start(ref, basis.at[i]) for i, ref in enumerate((basis_0_ref, basis_1_ref, base_ref))]
     others += [copies.start(side_ref.at[part], images.at[part, :R]) for part in range(2)]
-    far = far_part(place_ref, ranks_ref, own_ref, partner_ref, rows, tiles, left)
+    far = far_part(place_ref, ranks_ref, own_ref, partner_ref, rows_copy, rows, tiles, left)
     wait(others)
     basis[2] = basis[2] + far
     sent = [copies.start(basis.at[2], basis_2_ref)]
@@ -252,10 +275,10 @@
     sums[2 * R : 4 * R] = total[:, R:]
     sums[4 * R :] = last[0] + last[1]
     z, core = place_ref[0], place_ref[1]
-    size = sums_ref.shape[2]
-    for d in range(2):
+    size = mine_ref.shape[1]
+    for d, ref in enumerate((mine_ref, other_ref)):
         for k in range(4):
-            sums_ref[d, k] = sums[aligned(4 * (core ^ d) + (z ^ k), size)]
+            ref[k] = sums[aligned(4 * (core ^ d) + (z ^ k), size)]
     wait(sent)
 
 
@@ -311,8 +334,8 @@
     return (x + one) + (two + three)
 
 
-def sum_halves(x):
-    total = x[0] + swap(x[1], "c", 1)
+def sum_halves(mine, other):
+    total = mine + swap(other, "c", 1)
     for axis in ("z", "y", "x"):
         total = sum_axis(total, axis)
     return total, swap(total, "c", 1)
@@ -323,8 +346,8 @@
     return own, swap(own, "c", 1)
 
 
-def sum_pieces(x):
-    pair = x[0] + swap(x[1], "c", 1)
+def sum_pieces(mine, other):
+    pair = mine + swap(other, "c", 1)
     one, two, three = (swap(pair[k], "z", k) for k in (1, 2, 3))
     total = (pair[0] + one) + (two + three)
     for axis in ("y", "x"):
@@ -342,9 +365,8 @@
     width = right_side.shape[2]
     sub_blocks = near_columns.shape[1]
     x, y, z, core = (lax.axis_index(axis) for axis in ALL)
-    place = jnp.stack([z, core]).astype(jnp.int32)
+    place = jnp.stack([z, core, 4 * x + y]).astype(jnp.int32)
     where = near_columns[0] - (2 * z + core) * sub_blocks + HALO
-    ranks = lax.dynamic_index_in_dim(tile_ranks, 4 * x + y, 0, keepdims=False)
     columns = column_factors[0].reshape(TILES * 2 * K, width)
     rows = row_factors[0].reshape(TILES * 2 * K, width)
     near = near_blocks[0]
@@ -362,7 +384,7 @@
     rounded_scratch = VMEM((2, R, width), jnp.bfloat16)
     products_scratch = VMEM((TILES, R, 2 * K), jnp.bfloat16)
     weights = VMEM((TILES * 2 * K, width), jnp.bfloat16)
-    far_scratch = [products_scratch, VMEM((2 * R, TILES * 2 * K), jnp.bfloat16)]
+    far_scratch = [products_scratch, VMEM((2 * R, TILES * 2 * K), jnp.bfloat16), weights]
     square = VMEM((R, R), jnp.float32)
     outer = VMEM((5 * R, R), jnp.float32)
     stacked = VMEM((2, 3 * R, width), jnp.float32)
@@ -402,29 +424,29 @@
         )
         return own, partner, base
 
-    (gram,) = call(
-        gram_kernel, ((shape(2, R // 2, R), WHOLE),), 1, 1, [square], 0, place, right_side, limit=SMALL
-    )
+    half = (shape(R // 2, R), WHOLE)
+    gram = call(gram_kernel, (half, half), 1, 1, [square], 0, place, right_side, limit=SMALL)
     operands = ((block, ANY), (rounded_block, ANY), (edge, ANY), (edge, ANY), (products_block, ANY))
     basis_0, *rest = call(
         start_kernel, operands, 1, 2, [square, wide, weights, wide, rounded_scratch, products_scratch], 10,
-        place, *sum_halves(gram), right_side, columns,
+        place, *sum_halves(*gram), right_side, columns,
     )
     own, partner, base = operate(basis_0, *rest)
     basis_1, *rest = call(
-        middle_kernel, operands, 2, 3, [*far_scratch, weights, wide, rounded_scratch, products_scratch], 10,
-        place, ranks, own, partner, rows, base, columns,
+        middle_kernel, operands, 2, 2, [*far_scratch, weights, wide, rounded_scratch, products_scratch], 11,
+        place, tile_ranks, own, partner, rows, base, columns,
     )
     own, partner, base = operate(basis_1, *rest)
-    basis_2, sums = call(
-        last_kernel, ((block, ANY), (shape(2, 4, 5 * R // 8, R), WHOLE)), 2, 3,
-        [*far_scratch, VMEM((3, 2, R, width), jnp.float32), stacked, outer], 6,
-        place, ranks, own, partner, rows, base, right_side, basis_0, basis_1,
+    pieces = (shape(4, 5 * R // 8, R), WHOLE)
+    basis_2, *sums = call(
+        last_kernel, ((block, ANY), pieces, pieces), 2, 2,
+        [*far_scratch, VMEM((3, 2, R, width), jnp.float32), stacked, outer], 7,
+        place, tile_ranks, own, partner, rows, base, right_side, basis_0, basis_1,
     )
     return call(
         finish_kernel, ((block, ANY), (block, ANY)), 1, 2,
         [outer, VMEM((2, R, R), jnp.float32), square, square, stacked, wide, wide, wide], 11,
-        place, *sum_pieces(sums), right_side, basis_0, basis_1, basis_2,
+        place, *sum_pieces(*sums), right_side, basis_0, basis_1, basis_2,
     )
 
 

time: 191 us -> 192 us (level)
  waiting for transfers between devices: 33.8 us -> 37.4 us
  Pallas kernels: 52.7 us -> 50.4 us
    ppermute x33, waiting for transfers between devices: 26.2 us -> 29 us  [swap(): return lax.ppermute(x, axis, [(i, i ^ k) for i in range(n)])]
    pallas_call x7, Pallas kernels: 52.7 us -> 50.4 us  [call(): pl.pallas_call(kernel, out_shape=tuple((kind for kind, _ in out_specs)),...]
    ppermute x33, starting transfers between devices: 46.5 us -> 48.7 us  [swap(): return lax.ppermute(x, axis, [(i, i ^ k) for i in range(n)])]
    unnamed x32 -> x30, local copies, waits for them, and re-layouts: 5.13 us -> 5.11 us
  transfers between devices with their start and end apart: 37 -> 37, of which waited for: 26 -> 29; matrix products, arithmetic and copies ran while one was open for 1% -> 0% of each run, Pallas kernels for 6% -> 6%
where the time goes in v1:
time: 192 us
  starting transfers between devices  58.4 us (30%)
  Pallas kernels  50.4 us (26%)
  waiting for transfers between devices  37.4 us (19%)
  blocking collectives  37.3 us (19%)
  local copies, waits for them, and re-layouts  5.12 us (3%)
    pallas_call x7, Pallas kernels, call(): pl.pallas_call(kernel, out_shape=tuple((kind for kind, _ in out_specs)),...  50.4 us
    ppermute x33, starting transfers between devices, swap(): return lax.ppermute(x, axis, [(i, i ^ k) for i in range(n)])  48.7 us
    all_to_all x2, blocking collectives, gather_coeffs(): lax.all_to_all(products.reshape(8 * TILES, 16, 2 * K), ALL, 0, 0, tiled=T...  37.3 us
    ppermute x33, waiting for transfers between devices, swap(): return lax.ppermute(x, axis, [(i, i ^ k) for i in range(n)])  29 us
    ppermute x2, waiting for transfers between devices, operate(): from_right = lax.ppermute(low, ('z', 'c'), backward)  8.03 us
    ppermute x2, starting transfers between devices, operate(): from_left = lax.ppermute(high, ('z', 'c'), forward)  5.71 us
    unnamed x30, local copies, waits for them, and re-layouts  5.11 us
    ppermute x2, starting transfers between devices, operate(): from_right = lax.ppermute(low, ('z', 'c'), backward)  4.02 us
  transfers between devices with their start and end apart: 37, of which 29 were waited for; matrix products, arithmetic and copies ran while one was open for 0% of the time, Pallas kernels for 6%

profile of v1, /device:TPU:1, one launch (start us, length us, event | category | flops | bytes accessed | tf_op | source)
XLA Modules:
  0.0 191.6 jit_solution(9765639540826356605)
XLA Ops:
  0.7 1.1 copy-done
  1.9 1.4 shard_map.86
  3.2 1.5 collective-permute-start
  4.7 0.9 collective-permute-done
  5.5 3.9 %collective-permute-start.3 = (f32[64,128]{1,0:T(8,128)S(1)}, f32[64,128]{1,0:T(8,128)S(1)}, u32[]{:S(2)}, u32[]{:S(2)}) collective-permute-start(f32[64,128]{1,0:T(8,128)S(1)} %add.75), channel_id=1, source_target_pairs={{0,6},{2,4},{4,2},{6,0},{1,7},{3,5},{5,3},{7,1},{8,14},{10,12},{12... | collective-permute-start | bytes 98312 | tf_op jit(solution)/shard_map/ppermute | solution.py:329
  9.4 0.7 collective-permute-start.1
  10.7 3.0 %collective-permute-done.2 = f32[64,128]{1,0:T(8,128)S(1)} collective-permute-done((f32[64,128]{1,0:T(8,128)S(1)}, f32[64,128]{1,0:T(8,128)S(1)}, u32[]{:S(2)}, u32[]{:S(2)}) %collective-permute-start.2) | collective-permute-done | bytes 32800 | tf_op jit(solution)/shard_map/ppermute | solution.py:329
  13.7 2.8 %collective-permute-start.6 = (f32[64,128]{1,0:T(8,128)S(1)}, f32[64,128]{1,0:T(8,128)S(1)}, u32[]{:S(2)}, u32[]{:S(2)}) collective-permute-start(f32[64,128]{1,0:T(8,128)S(1)} %add_add_fusion.4), channel_id=1, source_target_pairs={{0,24},{8,16},{16,8},{24,0},{1,25},{9,17},{17,9},{25,1},{2,26},{10... | collective-permute-start | bytes 98312 | tf_op jit(solution)/shard_map/ppermute | solution.py:329
  17.8 3.0 %collective-permute-done.5 = f32[64,128]{1,0:T(8,128)S(1)} collective-permute-done((f32[64,128]{1,0:T(8,128)S(1)}, f32[64,128]{1,0:T(8,128)S(1)}, u32[]{:S(2)}, u32[]{:S(2)}) %collective-permute-start.5) | collective-permute-done | bytes 32800 | tf_op jit(solution)/shard_map/ppermute | solution.py:329
  20.8 2.6 %collective-permute-start.9 = (f32[64,128]{1,0:T(8,128)S(1)}, f32[64,128]{1,0:T(8,128)S(1)}, u32[]{:S(2)}, u32[]{:S(2)}) collective-permute-start(f32[64,128]{1,0:T(8,128)S(1)} %add_add_fusion.3), channel_id=1, source_target_pairs={{0,96},{32,64},{64,32},{96,0},{1,97},{33,65},{65,33},{97,1},{2,98}... | collective-permute-start | bytes 98312 | tf_op jit(solution)/shard_map/ppermute | solution.py:329
  24.1 0.7 collective-permute-done.9
  24.9 2.8 %collective-permute-done.8 = f32[64,128]{1,0:T(8,128)S(1)} collective-permute-done((f32[64,128]{1,0:T(8,128)S(1)}, f32[64,128]{1,0:T(8,128)S(1)}, u32[]{:S(2)}, u32[]{:S(2)}) %collective-permute-start.8) | collective-permute-done | bytes 32800 | tf_op jit(solution)/shard_map/ppermute | solution.py:329
  27.7 4.7 %collective-permute-start.10 = (f32[64,128]{1,0:T(8,128)S(1)}, f32[64,128]{1,0:T(8,128)S(1)}, u32[]{:S(2)}, u32[]{:S(2)}) collective-permute-start(f32[64,128]{1,0:T(8,128)S(1)} %add_add_fusion.2.mine_ref), channel_id=1, source_target_pairs={{0,1},{1,0},{2,3},{3,2},{4,5},{5,4},{6,7},{7,6},{8,9},{9,8},{10,11... | collective-permute-start | bytes 98312 | tf_op jit(solution)/shard_map/ppermute | solution.py:329
  32.4 0.9 collective-permute-done.10.other_ref
  33.8 8.6 %shard_map.87 = (f32[2,128,768]{2,1,0:T(8,128)}, bf16[2,128,768]{2,1,0:T(8,128)(2,1)}, bf16[2,128,256]{2,1,0:T(8,128)(2,1)}, bf16[2,128,256]{2,1,0:T(8,128)(2,1)}, bf16[16,128,128]{2,1,0:T(8,128)(2,1)}) custom-call(s32[3]{0:T(128)} %copy-done.1, f32[64,128]{1,0:T(8,128)} %copy-done.8, f32[64,128]{1,0:T(8,128)} %copy-done.13, f32[2,128,768]{2,1,0:T(8,128)} %side_ref.7, ...), custom_call_target="tpu_custom_call" | custom-call | flops 300000000 | bytes 6291456 | tf_op jit(solution)/shard_map/pallas_call | solution.py:395
  42.5 19.7 %all_to_all.10 = bf16[128,16,128]{2,1,0:T(8,128)(2,1)S(1)} all-to-all(bf16[128,16,128]{2,1,0:T(8,128)(2,1)} %bitcast.45), channel_id=1, replica_groups=mesh['x'=4,'y'=4,'z'=4,'c'=2] {'x','y','z','c'}, dimensions={0} | all-to-all | bytes 1048576 | tf_op jit(solution)/shard_map/all_to_all | solution.py:359
  62.2 0.9 collective-permute-start.13
  63.2 0.7 collective-permute-start.12
  63.8 1.7 collective-permute-start.11
  65.6 1.1 collective-permute-done.13
  66.6 1.1 collective-permute-done.12
  68.3 2.5 %collective-permute-start.14 = (bf16[4,16,16,128]{3,2,1,0:T(8,128)(2,1)S(1)}, bf16[4,16,16,128]{3,2,1,0:T(8,128)(2,1)S(1)}, u32[]{:S(2)}, u32[]{:S(2)}) collective-permute-start(bf16[4,16,16,128]{3,2,1,0:T(8,128)(2,1)S(1)} %pad_maximum_fusion.own_ref), channel_id=1, source_target_pairs={{0,1},{1,0},{2,3},{3,2},{4,5},{5,4},{6,7},{7,6},{8,9},{9,8},{10,11... | collective-permute-start | bytes 786440 | tf_op jit(solution)/shard_map/ppermute | solution.py:329
  70.7 2.9 %collective-permute-start.15 = (bf16[2,128,256]{2,1,0:T(8,128)(2,1)}, bf16[2,128,256]{2,1,0:T(8,128)(2,1)S(1)}, u32[]{:S(2)}, u32[]{:S(2)}) collective-permute-start(bf16[2,128,256]{2,1,0:T(8,128)(2,1)} %get-tuple-element.22), channel_id=1, source_target_pairs={{0,1},{1,2},{2,3},{3,4},{4,5},{5,6},{6,7},{8,9},{9,10},{10,11},{11... | collective-permute-start | bytes 393224 | tf_op jit(solution)/shard_map/ppermute | solution.py:407
  73.6 2.1 %collective-permute-start.16 = (bf16[2,128,256]{2,1,0:T(8,128)(2,1)}, bf16[2,128,256]{2,1,0:T(8,128)(2,1)S(1)}, u32[]{:S(2)}, u32[]{:S(2)}) collective-permute-start(bf16[2,128,256]{2,1,0:T(8,128)(2,1)} %get-tuple-element.23), channel_id=1, source_target_pairs={{1,0},{2,1},{3,2},{4,3},{5,4},{6,5},{7,6},{9,8},{10,9},{11,10},{12... | collective-permute-start | bytes 393224 | tf_op jit(solution)/shard_map/ppermute | solution.py:406
  76.3 3.8 %collective-permute-done.16.high_ref = bf16[2,128,256]{2,1,0:T(8,128)(2,1)S(1)} collective-permute-done((bf16[2,128,256]{2,1,0:T(8,128)(2,1)}, bf16[2,128,256]{2,1,0:T(8,128)(2,1)S(1)}, u32[]{:S(2)}, u32[]{:S(2)}) %collective-permute-start.16) | collective-permute-done | bytes 131104 | tf_op jit(solution)/shard_map/ppermute | solution.py:406
  80.8 6.1 %shard_map.88.base_ref = f32[2,128,768]{2,1,0:T(8,128)} custom-call(s32[6,6]{1,0:T(8,128)} %fusion.3.where_ref, f32[2,128,768]{2,1,0:T(8,128)} %get-tuple-element.20.x_ref.basis_0_ref, bf16[2,128,768]{2,1,0:T(8,128)(2,1)} %get-tuple-element.21.rounded_ref, bf16[2,128,256]{2,1,0:T(8,128)(2,1)} %copy-done.9, bf16[2,128,256]{2,1,0:T(8,128)(2,1)} %copy-done.11, ...), custom_call_target="tpu_custom_call" | custom-call | flops 300000000 | bytes 6291456 | tf_op jit(solution)/shard_map/pallas_call | solution.py:395
  86.9 0.7 copy-done.5
  87.6 6.4 %shard_map.89 = (f32[2,128,768]{2,1,0:T(8,128)}, bf16[2,128,768]{2,1,0:T(8,128)(2,1)}, bf16[2,128,256]{2,1,0:T(8,128)(2,1)}, bf16[2,128,256]{2,1,0:T(8,128)(2,1)}, bf16[16,128,128]{2,1,0:T(8,128)(2,1)}) custom-call(s32[3]{0:T(128)} %copy-done.1, s32[16,16]{1,0:T(8,128)} %ranks_ref.3, bf16[4,16,16,128]{3,2,1,0:T(8,128)(2,1)} %copy-done.2, ...), custom_call_target="tpu_custom_call" | custom-call | flops 300000000 | bytes 6291456 | tf_op jit(solution)/shard_map/pallas_call | solution.py:395
  94.0 17.6 %all_to_all.11 = bf16[128,16,128]{2,1,0:T(8,128)(2,1)S(1)} all-to-all(bf16[128,16,128]{2,1,0:T(8,128)(2,1)} %bitcast.44), channel_id=1, replica_groups=mesh['x'=4,'y'=4,'z'=4,'c'=2] {'x','y','z','c'}, dimensions={0} | all-to-all | bytes 1048576 | tf_op jit(solution)/shard_map/all_to_all | solution.py:359
  111.7 0.9 collective-permute-start.19
  112.6 0.7 collective-permute-start.18
  113.3 1.7 collective-permute-start.17
  115.0 1.1 collective-permute-done.19
  116.1 1.1 collective-permute-done.18
  117.7 2.5 %collective-permute-start.20 = (bf16[4,16,16,128]{3,2,1,0:T(8,128)(2,1)S(1)}, bf16[4,16,16,128]{3,2,1,0:T(8,128)(2,1)S(1)}, u32[]{:S(2)}, u32[]{:S(2)}) collective-permute-start(bf16[4,16,16,128]{3,2,1,0:T(8,128)(2,1)S(1)} %pad_maximum_fusion.1.own_ref), channel_id=1, source_target_pairs={{0,1},{1,0},{2,3},{3,2},{4,5},{5,4},{6,7},{7,6},{8,9},{9,8},{10,11... | collective-permute-start | bytes 786440 | tf_op jit(solution)/shard_map/ppermute | solution.py:329
  120.2 2.9 %collective-permute-start.21 = (bf16[2,128,256]{2,1,0:T(8,128)(2,1)}, bf16[2,128,256]{2,1,0:T(8,128)(2,1)S(1)}, u32[]{:S(2)}, u32[]{:S(2)}) collective-permute-start(bf16[2,128,256]{2,1,0:T(8,128)(2,1)} %get-tuple-element.27), channel_id=1, source_target_pairs={{0,1},{1,2},{2,3},{3,4},{4,5},{5,6},{6,7},{8,9},{9,10},{10,11},{11... | collective-permute-start | bytes 393224 | tf_op jit(solution)/shard_map/ppermute | solution.py:407
  123.1 1.9 %collective-permute-start.22 = (bf16[2,128,256]{2,1,0:T(8,128)(2,1)}, bf16[2,128,256]{2,1,0:T(8,128)(2,1)S(1)}, u32[]{:S(2)}, u32[]{:S(2)}) collective-permute-start(bf16[2,128,256]{2,1,0:T(8,128)(2,1)} %get-tuple-element.28), channel_id=1, source_target_pairs={{1,0},{2,1},{3,2},{4,3},{5,4},{6,5},{7,6},{9,8},{10,9},{11,10},{12... | collective-permute-start | bytes 393224 | tf_op jit(solution)/shard_map/ppermute | solution.py:406
  125.3 4.3 %collective-permute-done.22.high_ref = bf16[2,128,256]{2,1,0:T(8,128)(2,1)S(1)} collective-permute-done((bf16[2,128,256]{2,1,0:T(8,128)(2,1)}, bf16[2,128,256]{2,1,0:T(8,128)(2,1)S(1)}, u32[]{:S(2)}, u32[]{:S(2)}) %collective-permute-start.22) | collective-permute-done | bytes 131104 | tf_op jit(solution)/shard_map/ppermute | solution.py:406
  130.2 6.1 %shard_map.90.base_ref = f32[2,128,768]{2,1,0:T(8,128)} custom-call(s32[6,6]{1,0:T(8,128)} %fusion.3.where_ref, f32[2,128,768]{2,1,0:T(8,128)} %get-tuple-element.25.x_ref.basis_1_ref, bf16[2,128,768]{2,1,0:T(8,128)(2,1)} %get-tuple-element.26.rounded_ref, bf16[2,128,256]{2,1,0:T(8,128)(2,1)} %copy-done.10, bf16[2,128,256]{2,1,0:T(8,128)(2,1)} %copy-done.12, ...), custom_call_target="tpu_custom_call" | custom-call | flops 300000000 | bytes 6291456 | tf_op jit(solution)/shard_map/pallas_call | solution.py:395
  136.3 0.7 copy-done.6
  137.0 8.1 %shard_map.91 = (f32[2,128,768]{2,1,0:T(8,128)}, f32[4,80,128]{2,1,0:T(8,128)}, f32[4,80,128]{2,1,0:T(8,128)}) custom-call(s32[3]{0:T(128)} %copy-done.1, s32[16,16]{1,0:T(8,128)} %ranks_ref.3, bf16[4,16,16,128]{3,2,1,0:T(8,128)(2,1)} %copy-done.3, bf16[4,16,16,128]{3,2,1,0:T(8,128)(2,1)} %copy-done.6, bf16[2048,768]{1,0:T(8,128)(2,1)} %bitcast.41, ...), custom_call_target="tpu_custom_call" | custom-call | flops 300000000 | bytes 6291456 | tf_op jit(solution)/shard_map/pallas_call | solution.py:395
  145.2 1.6 collective-permute-done.23
  146.8 0.9 add.89
  148.2 1.5 collective-permute-start.25
  149.8 1.3 collective-permute-start.24
  151.1 0.8 collective-permute-done.26
  151.9 0.8 collective-permute-done.25
  153.5 1.9 collective-permute-start.28
  155.4 1.2 collective-permute-start.27
  156.6 0.8 collective-permute-done.29
  158.4 0.9 collective-permute-start.32
  159.3 1.2 collective-permute-start.31
  160.6 1.2 collective-permute-start.30
  161.7 0.8 collective-permute-done.32
  162.6 1.2 collective-permute-done.31
  163.7 1.7 collective-permute-start.35
  165.5 0.9 collective-permute-start.34
  166.3 0.7 collective-permute-start.33
  167.1 0.8 collective-permute-done.35
  167.9 2.0 %collective-permute-done.34 = f32[80,128]{1,0:T(8,128)S(1)} collective-permute-done((f32[80,128]{1,0:T(8,128)S(1)}, f32[80,128]{1,0:T(8,128)S(1)}, u32[]{:S(2)}, u32[]{:S(2)}) %collective-permute-start.34) | collective-permute-done | bytes 40992 | tf_op jit(solution)/shard_map/ppermute | solution.py:329
  169.9 6.2 %collective-permute-start.36 = (f32[4,80,128]{2,1,0:T(8,128)S(1)}, f32[4,80,128]{2,1,0:T(8,128)S(1)}, u32[]{:S(2)}, u32[]{:S(2)}) collective-permute-start(f32[4,80,128]{2,1,0:T(8,128)S(1)} %pad_maximum_fusion.2.own_ref), channel_id=1, source_target_pairs={{0,1},{1,0},{2,3},{3,2},{4,5},{5,4},{6,7},{7,6},{8,9},{9,8},{10,11... | collective-permute-start | bytes 491528 | tf_op jit(solution)/shard_map/ppermute | solution.py:329
  176.0 1.0 collective-permute-done.36.partner_ref
  177.0 0.7 copy-done.7
  177.7 13.7 %shard_map.92 = (f32[2,128,768]{2,1,0:T(8,128)}, f32[2,128,768]{2,1,0:T(8,128)}) custom-call(s32[3]{0:T(128)} %copy-done.1, f32[4,80,128]{2,1,0:T(8,128)} %copy-done.4, f32[4,80,128]{2,1,0:T(8,128)} %copy-done.7, f32[2,128,768]{2,1,0:T(8,128)} %side_ref.7, f32[2,128,768]{2,1,0:T(8,128)} %get-tuple-element.20.x_ref.basis_0_ref, ...), custom_call_target="tpu_custom_call" | custom-call | flops 300000000 | bytes 6291456 | tf_op jit(solution)/shard_map/pallas_call | solution.py:395
  (65 shorter events, 9.2 us)
Async XLA Ops:
  0.7 1.1 copy-start
  1.8 31.4 %copy-start.1 = (s32[3]{0:T(128)}, s32[3]{0:T(128)S(1)}, u32[]{:S(2)}) copy-start(s32[3]{0:T(128)S(1)} %pad_add_fusion.place_ref) | copy-start | bytes 40
  3.2 2.3 %collective-permute-start = (f32[64,128]{1,0:T(8,128)S(1)}, f32[64,128]{1,0:T(8,128)S(1)}, u32[]{:S(2)}, u32[]{:S(2)}) collective-permute-start(f32[64,128]{1,0:T(8,128)S(1)} %get-tuple-element.18), channel_id=1, source_target_pairs={{0,1},{1,0},{2,3},{3,2},{4,5},{5,4},{6,7},{7,6},{8,9},{9,8},{10,11... | collective-permute-start | bytes 98312 | tf_op jit(solution)/shard_map/ppermute | solution.py:329
  5.5 5.2 %collective-permute-start.3 = (f32[64,128]{1,0:T(8,128)S(1)}, f32[64,128]{1,0:T(8,128)S(1)}, u32[]{:S(2)}, u32[]{:S(2)}) collective-permute-start(f32[64,128]{1,0:T(8,128)S(1)} %add.75), channel_id=1, source_target_pairs={{0,6},{2,4},{4,2},{6,0},{1,7},{3,5},{5,3},{7,1},{8,14},{10,12},{12... | collective-permute-start | bytes 98312 | tf_op jit(solution)/shard_map/ppermute | solution.py:329
  9.4 4.3 %collective-permute-start.2 = (f32[64,128]{1,0:T(8,128)S(1)}, f32[64,128]{1,0:T(8,128)S(1)}, u32[]{:S(2)}, u32[]{:S(2)}) collective-permute-start(f32[64,128]{1,0:T(8,128)S(1)} %add.75), channel_id=1, source_target_pairs={{0,4},{2,6},{4,0},{6,2},{1,5},{3,7},{5,1},{7,3},{8,12},{10,14},{12... | collective-permute-start | bytes 98312 | tf_op jit(solution)/shard_map/ppermute | solution.py:329
  9.4 4.3 %collective-permute-start.1 = (f32[64,128]{1,0:T(8,128)S(1)}, f32[64,128]{1,0:T(8,128)S(1)}, u32[]{:S(2)}, u32[]{:S(2)}) collective-permute-start(f32[64,128]{1,0:T(8,128)S(1)} %add.75), channel_id=1, source_target_pairs={{0,2},{2,0},{4,6},{6,4},{1,3},{3,1},{5,7},{7,5},{8,10},{10,8},{12,... | collective-permute-start | bytes 98312 | tf_op jit(solution)/shard_map/ppermute | solution.py:329
  13.7 4.1 %collective-permute-start.6 = (f32[64,128]{1,0:T(8,128)S(1)}, f32[64,128]{1,0:T(8,128)S(1)}, u32[]{:S(2)}, u32[]{:S(2)}) collective-permute-start(f32[64,128]{1,0:T(8,128)S(1)} %add_add_fusion.4), channel_id=1, source_target_pairs={{0,24},{8,16},{16,8},{24,0},{1,25},{9,17},{17,9},{25,1},{2,26},{10... | collective-permute-start | bytes 98312 | tf_op jit(solution)/shard_map/ppermute | solution.py:329
  16.5 4.3 %collective-permute-start.5 = (f32[64,128]{1,0:T(8,128)S(1)}, f32[64,128]{1,0:T(8,128)S(1)}, u32[]{:S(2)}, u32[]{:S(2)}) collective-permute-start(f32[64,128]{1,0:T(8,128)S(1)} %add_add_fusion.4), channel_id=1, source_target_pairs={{0,16},{8,24},{16,0},{24,8},{1,17},{9,25},{17,1},{25,9},{2,18},{10... | collective-permute-start | bytes 98312 | tf_op jit(solution)/shard_map/ppermute | solution.py:329
  16.9 3.9 %collective-permute-start.4 = (f32[64,128]{1,0:T(8,128)S(1)}, f32[64,128]{1,0:T(8,128)S(1)}, u32[]{:S(2)}, u32[]{:S(2)}) collective-permute-start(f32[64,128]{1,0:T(8,128)S(1)} %add_add_fusion.4), channel_id=1, source_target_pairs={{0,8},{8,0},{16,24},{24,16},{1,9},{9,1},{17,25},{25,17},{2,10},{10... | collective-permute-start | bytes 98312 | tf_op jit(solution)/shard_map/ppermute | solution.py:329
  20.8 54.9 %copy-start.14 = (s32[1,6,6]{2,0,1:T(1,128)S(1)}, s32[1,6,6]{2,0,1:T(1,128)}, u32[]{:S(2)}) copy-start(s32[1,6,6]{2,0,1:T(1,128)} %param.10) | copy-start | bytes 436
  20.8 4.1 %collective-permute-start.9 = (f32[64,128]{1,0:T(8,128)S(1)}, f32[64,128]{1,0:T(8,128)S(1)}, u32[]{:S(2)}, u32[]{:S(2)}) collective-permute-start(f32[64,128]{1,0:T(8,128)S(1)} %add_add_fusion.3), channel_id=1, source_target_pairs={{0,96},{32,64},{64,32},{96,0},{1,97},{33,65},{65,33},{97,1},{2,98}... | collective-permute-start | bytes 98312 | tf_op jit(solution)/shard_map/ppermute | solution.py:329
  23.4 4.3 %collective-permute-start.8 = (f32[64,128]{1,0:T(8,128)S(1)}, f32[64,128]{1,0:T(8,128)S(1)}, u32[]{:S(2)}, u32[]{:S(2)}) collective-permute-start(f32[64,128]{1,0:T(8,128)S(1)} %add_add_fusion.3), channel_id=1, source_target_pairs={{0,64},{32,96},{64,0},{96,32},{1,65},{33,97},{65,1},{97,33},{2,66}... | collective-permute-start | bytes 98312 | tf_op jit(solution)/shard_map/ppermute | solution.py:329
  23.9 3.8 %collective-permute-start.7 = (f32[64,128]{1,0:T(8,128)S(1)}, f32[64,128]{1,0:T(8,128)S(1)}, u32[]{:S(2)}, u32[]{:S(2)}) collective-permute-start(f32[64,128]{1,0:T(8,128)S(1)} %add_add_fusion.3), channel_id=1, source_target_pairs={{0,32},{32,0},{64,96},{96,64},{1,33},{33,1},{65,97},{97,65},{2,34}... | collective-permute-start | bytes 98312 | tf_op jit(solution)/shard_map/ppermute | solution.py:329
  27.6 5.6 %copy-start.8 = (f32[64,128]{1,0:T(8,128)}, f32[64,128]{1,0:T(8,128)S(1)}, u32[]{:S(2)}) copy-start(f32[64,128]{1,0:T(8,128)S(1)} %add_add_fusion.2.mine_ref) | copy-start | bytes 98308
  27.7 5.6 %collective-permute-start.10 = (f32[64,128]{1,0:T(8,128)S(1)}, f32[64,128]{1,0:T(8,128)S(1)}, u32[]{:S(2)}, u32[]{:S(2)}) collective-permute-start(f32[64,128]{1,0:T(8,128)S(1)} %add_add_fusion.2.mine_ref), channel_id=1, source_target_pairs={{0,1},{1,0},{2,3},{3,2},{4,5},{5,4},{6,7},{7,6},{8,9},{9,8},{10,11... | collective-permute-start | bytes 98312 | tf_op jit(solution)/shard_map/ppermute | solution.py:329
  33.2 0.6 copy-start.13
  62.2 4.4 %collective-permute-start.13 = (bf16[16,16,128]{2,1,0:T(8,128)(2,1)S(1)}, bf16[16,16,128]{2,1,0:T(8,128)(2,1)S(1)}, u32[]{:S(2)}, u32[]{:S(2)}) collective-permute-start(bf16[16,16,128]{2,1,0:T(8,128)(2,1)S(1)} %bitcast_reduce_fusion.1), channel_id=1, source_target_pairs={{0,6},{2,4},{4,2},{6,0},{1,7},{3,5},{5,3},{7,1},{8,14},{10,12},{12... | collective-permute-start | bytes 196616 | tf_op jit(solution)/shard_map/ppermute | solution.py:329
  63.2 4.6 %collective-permute-start.12 = (bf16[16,16,128]{2,1,0:T(8,128)(2,1)S(1)}, bf16[16,16,128]{2,1,0:T(8,128)(2,1)S(1)}, u32[]{:S(2)}, u32[]{:S(2)}) collective-permute-start(bf16[16,16,128]{2,1,0:T(8,128)(2,1)S(1)} %bitcast_reduce_fusion.1), channel_id=1, source_target_pairs={{0,4},{2,6},{4,0},{6,2},{1,5},{3,7},{5,1},{7,3},{8,12},{10,14},{12... | collective-permute-start | bytes 196616 | tf_op jit(solution)/shard_map/ppermute | solution.py:329
  63.8 4.4 %collective-permute-start.11 = (bf16[16,16,128]{2,1,0:T(8,128)(2,1)S(1)}, bf16[16,16,128]{2,1,0:T(8,128)(2,1)S(1)}, u32[]{:S(2)}, u32[]{:S(2)}) collective-permute-start(bf16[16,16,128]{2,1,0:T(8,128)(2,1)S(1)} %bitcast_reduce_fusion.1), channel_id=1, source_target_pairs={{0,2},{2,0},{4,6},{6,4},{1,3},{3,1},{5,7},{7,5},{8,10},{10,8},{12,... | collective-permute-start | bytes 196616 | tf_op jit(solution)/shard_map/ppermute | solution.py:329
  68.3 18.6 %copy-start.2 = (bf16[4,16,16,128]{3,2,1,0:T(8,128)(2,1)}, bf16[4,16,16,128]{3,2,1,0:T(8,128)(2,1)S(1)}, u32[]{:S(2)}) copy-start(bf16[4,16,16,128]{3,2,1,0:T(8,128)(2,1)S(1)} %pad_maximum_fusion.own_ref) | copy-start | bytes 786436
  68.3 18.6 %collective-permute-start.14 = (bf16[4,16,16,128]{3,2,1,0:T(8,128)(2,1)S(1)}, bf16[4,16,16,128]{3,2,1,0:T(8,128)(2,1)S(1)}, u32[]{:S(2)}, u32[]{:S(2)}) collective-permute-start(bf16[4,16,16,128]{3,2,1,0:T(8,128)(2,1)S(1)} %pad_maximum_fusion.own_ref), channel_id=1, source_target_pairs={{0,1},{1,0},{2,3},{3,2},{4,5},{5,4},{6,7},{7,6},{8,9},{9,8},{10,11... | collective-permute-start | bytes 786440 | tf_op jit(solution)/shard_map/ppermute | solution.py:329
  70.7 5.6 %collective-permute-start.15 = (bf16[2,128,256]{2,1,0:T(8,128)(2,1)}, bf16[2,128,256]{2,1,0:T(8,128)(2,1)S(1)}, u32[]{:S(2)}, u32[]{:S(2)}) collective-permute-start(bf16[2,128,256]{2,1,0:T(8,128)(2,1)} %get-tuple-element.22), channel_id=1, source_target_pairs={{0,1},{1,2},{2,3},{3,4},{4,5},{5,6},{6,7},{8,9},{9,10},{10,11},{11... | collective-permute-start | bytes 393224 | tf_op jit(solution)/shard_map/ppermute | solution.py:407
  73.6 6.5 %collective-permute-start.16 = (bf16[2,128,256]{2,1,0:T(8,128)(2,1)}, bf16[2,128,256]{2,1,0:T(8,128)(2,1)S(1)}, u32[]{:S(2)}, u32[]{:S(2)}) collective-permute-start(bf16[2,128,256]{2,1,0:T(8,128)(2,1)} %get-tuple-element.23), channel_id=1, source_target_pairs={{1,0},{2,1},{3,2},{4,3},{5,4},{6,5},{7,6},{9,8},{10,9},{11,10},{12... | collective-permute-start | bytes 393224 | tf_op jit(solution)/shard_map/ppermute | solution.py:406
  76.3 3.8 %copy-start.9 = (bf16[2,128,256]{2,1,0:T(8,128)(2,1)}, bf16[2,128,256]{2,1,0:T(8,128)(2,1)S(1)}, u32[]{:S(2)}) copy-start(bf16[2,128,256]{2,1,0:T(8,128)(2,1)S(1)} %collective-permute-done.15.low_ref) | copy-start | bytes 393220
  80.1 0.6 copy-start.11
  86.8 0.7 copy-start.5
  111.7 4.4 %collective-permute-start.19 = (bf16[16,16,128]{2,1,0:T(8,128)(2,1)S(1)}, bf16[16,16,128]{2,1,0:T(8,128)(2,1)S(1)}, u32[]{:S(2)}, u32[]{:S(2)}) collective-permute-start(bf16[16,16,128]{2,1,0:T(8,128)(2,1)S(1)} %bitcast_reduce_fusion), channel_id=1, source_target_pairs={{0,6},{2,4},{4,2},{6,0},{1,7},{3,5},{5,3},{7,1},{8,14},{10,12},{12... | collective-permute-start | bytes 196616 | tf_op jit(solution)/shard_map/ppermute | solution.py:329
  112.6 4.6 %collective-permute-start.18 = (bf16[16,16,128]{2,1,0:T(8,128)(2,1)S(1)}, bf16[16,16,128]{2,1,0:T(8,128)(2,1)S(1)}, u32[]{:S(2)}, u32[]{:S(2)}) collective-permute-start(bf16[16,16,128]{2,1,0:T(8,128)(2,1)S(1)} %bitcast_reduce_fusion), channel_id=1, source_target_pairs={{0,4},{2,6},{4,0},{6,2},{1,5},{3,7},{5,1},{7,3},{8,12},{10,14},{12... | collective-permute-start | bytes 196616 | tf_op jit(solution)/shard_map/ppermute | solution.py:329
  113.3 4.4 %collective-permute-start.17 = (bf16[16,16,128]{2,1,0:T(8,128)(2,1)S(1)}, bf16[16,16,128]{2,1,0:T(8,128)(2,1)S(1)}, u32[]{:S(2)}, u32[]{:S(2)}) collective-permute-start(bf16[16,16,128]{2,1,0:T(8,128)(2,1)S(1)} %bitcast_reduce_fusion), channel_id=1, source_target_pairs={{0,2},{2,0},{4,6},{6,4},{1,3},{3,1},{5,7},{7,5},{8,10},{10,8},{12,... | collective-permute-start | bytes 196616 | tf_op jit(solution)/shard_map/ppermute | solution.py:329
  117.7 18.6 %copy-start.3 = (bf16[4,16,16,128]{3,2,1,0:T(8,128)(2,1)}, bf16[4,16,16,128]{3,2,1,0:T(8,128)(2,1)S(1)}, u32[]{:S(2)}) copy-start(bf16[4,16,16,128]{3,2,1,0:T(8,128)(2,1)S(1)} %pad_maximum_fusion.1.own_ref) | copy-start | bytes 786436
  117.7 18.6 %collective-permute-start.20 = (bf16[4,16,16,128]{3,2,1,0:T(8,128)(2,1)S(1)}, bf16[4,16,16,128]{3,2,1,0:T(8,128)(2,1)S(1)}, u32[]{:S(2)}, u32[]{:S(2)}) collective-permute-start(bf16[4,16,16,128]{3,2,1,0:T(8,128)(2,1)S(1)} %pad_maximum_fusion.1.own_ref), channel_id=1, source_target_pairs={{0,1},{1,0},{2,3},{3,2},{4,5},{5,4},{6,7},{7,6},{8,9},{9,8},{10,11... | collective-permute-start | bytes 786440 | tf_op jit(solution)/shard_map/ppermute | solution.py:329
  120.2 5.1 %collective-permute-start.21 = (bf16[2,128,256]{2,1,0:T(8,128)(2,1)}, bf16[2,128,256]{2,1,0:T(8,128)(2,1)S(1)}, u32[]{:S(2)}, u32[]{:S(2)}) collective-permute-start(bf16[2,128,256]{2,1,0:T(8,128)(2,1)} %get-tuple-element.27), channel_id=1, source_target_pairs={{0,1},{1,2},{2,3},{3,4},{4,5},{5,6},{6,7},{8,9},{9,10},{10,11},{11... | collective-permute-start | bytes 393224 | tf_op jit(solution)/shard_map/ppermute | solution.py:407
  123.1 6.5 %collective-permute-start.22 = (bf16[2,128,256]{2,1,0:T(8,128)(2,1)}, bf16[2,128,256]{2,1,0:T(8,128)(2,1)S(1)}, u32[]{:S(2)}, u32[]{:S(2)}) collective-permute-start(bf16[2,128,256]{2,1,0:T(8,128)(2,1)} %get-tuple-element.28), channel_id=1, source_target_pairs={{1,0},{2,1},{3,2},{4,3},{5,4},{6,5},{7,6},{9,8},{10,9},{11,10},{12... | collective-permute-start | bytes 393224 | tf_op jit(solution)/shard_map/ppermute | solution.py:406
  125.3 4.3 %copy-start.10 = (bf16[2,128,256]{2,1,0:T(8,128)(2,1)}, bf16[2,128,256]{2,1,0:T(8,128)(2,1)S(1)}, u32[]{:S(2)}) copy-start(bf16[2,128,256]{2,1,0:T(8,128)(2,1)S(1)} %collective-permute-done.21.low_ref) | copy-start | bytes 393220
  129.6 0.7 copy-start.12
  136.3 0.7 copy-start.6
  145.1 1.7 collective-permute-start.23
  147.8 4.1 %collective-permute-start.26 = (f32[80,128]{1,0:T(8,128)S(1)}, f32[80,128]{1,0:T(8,128)S(1)}, u32[]{:S(2)}, u32[]{:S(2)}) collective-permute-start(f32[80,128]{1,0:T(8,128)S(1)} %get-tuple-element.32), channel_id=1, source_target_pairs={{0,6},{2,4},{4,2},{6,0},{1,7},{3,5},{5,3},{7,1},{8,14},{10,12},{12... | collective-permute-start | bytes 122888 | tf_op jit(solution)/shard_map/ppermute | solution.py:329
  148.2 4.5 %collective-permute-start.25 = (f32[80,128]{1,0:T(8,128)S(1)}, f32[80,128]{1,0:T(8,128)S(1)}, u32[]{:S(2)}, u32[]{:S(2)}) collective-permute-start(f32[80,128]{1,0:T(8,128)S(1)} %get-tuple-element.33), channel_id=1, source_target_pairs={{0,4},{2,6},{4,0},{6,2},{1,5},{3,7},{5,1},{7,3},{8,12},{10,14},{12... | collective-permute-start | bytes 122888 | tf_op jit(solution)/shard_map/ppermute | solution.py:329
  149.8 3.4 %collective-permute-start.24 = (f32[80,128]{1,0:T(8,128)S(1)}, f32[80,128]{1,0:T(8,128)S(1)}, u32[]{:S(2)}, u32[]{:S(2)}) collective-permute-start(f32[80,128]{1,0:T(8,128)S(1)} %get-tuple-element.34), channel_id=1, source_target_pairs={{0,2},{2,0},{4,6},{6,4},{1,3},{3,1},{5,7},{7,5},{8,10},{10,8},{12,... | collective-permute-start | bytes 122888 | tf_op jit(solution)/shard_map/ppermute | solution.py:329
  153.2 4.1 %collective-permute-start.29 = (f32[80,128]{1,0:T(8,128)S(1)}, f32[80,128]{1,0:T(8,128)S(1)}, u32[]{:S(2)}, u32[]{:S(2)}) collective-permute-start(f32[80,128]{1,0:T(8,128)S(1)} %fusion.1), channel_id=1, source_target_pairs={{0,24},{8,16},{16,8},{24,0},{1,25},{9,17},{17,9},{25,1},{2,26},{10... | collective-permute-start | bytes 122888 | tf_op jit(solution)/shard_map/ppermute | solution.py:329
  153.5 4.4 %collective-permute-start.28 = (f32[80,128]{1,0:T(8,128)S(1)}, f32[80,128]{1,0:T(8,128)S(1)}, u32[]{:S(2)}, u32[]{:S(2)}) collective-permute-start(f32[80,128]{1,0:T(8,128)S(1)} %fusion.1), channel_id=1, source_target_pairs={{0,16},{8,24},{16,0},{24,8},{1,17},{9,25},{17,1},{25,9},{2,18},{10... | collective-permute-start | bytes 122888 | tf_op jit(solution)/shard_map/ppermute | solution.py:329
  155.4 3.0 %collective-permute-start.27 = (f32[80,128]{1,0:T(8,128)S(1)}, f32[80,128]{1,0:T(8,128)S(1)}, u32[]{:S(2)}, u32[]{:S(2)}) collective-permute-start(f32[80,128]{1,0:T(8,128)S(1)} %fusion.1), channel_id=1, source_target_pairs={{0,8},{8,0},{16,24},{24,16},{1,9},{9,1},{17,25},{25,17},{2,10},{10... | collective-permute-start | bytes 122888 | tf_op jit(solution)/shard_map/ppermute | solution.py:329
  158.4 4.1 %collective-permute-start.32 = (f32[80,128]{1,0:T(8,128)S(1)}, f32[80,128]{1,0:T(8,128)S(1)}, u32[]{:S(2)}, u32[]{:S(2)}) collective-permute-start(f32[80,128]{1,0:T(8,128)S(1)} %add_add_fusion.1), channel_id=1, source_target_pairs={{0,96},{32,64},{64,32},{96,0},{1,97},{33,65},{65,33},{97,1},{2,98}... | collective-permute-start | bytes 122888 | tf_op jit(solution)/shard_map/ppermute | solution.py:329
  159.3 4.4 %collective-permute-start.31 = (f32[80,128]{1,0:T(8,128)S(1)}, f32[80,128]{1,0:T(8,128)S(1)}, u32[]{:S(2)}, u32[]{:S(2)}) collective-permute-start(f32[80,128]{1,0:T(8,128)S(1)} %add_add_fusion.1), channel_id=1, source_target_pairs={{0,64},{32,96},{64,0},{96,32},{1,65},{33,97},{65,1},{97,33},{2,66}... | collective-permute-start | bytes 122888 | tf_op jit(solution)/shard_map/ppermute | solution.py:329
  160.6 3.1 %collective-permute-start.30 = (f32[80,128]{1,0:T(8,128)S(1)}, f32[80,128]{1,0:T(8,128)S(1)}, u32[]{:S(2)}, u32[]{:S(2)}) collective-permute-start(f32[80,128]{1,0:T(8,128)S(1)} %add_add_fusion.1), channel_id=1, source_target_pairs={{0,32},{32,0},{64,96},{96,64},{1,33},{33,1},{65,97},{97,65},{2,34}... | collective-permute-start | bytes 122888 | tf_op jit(solution)/shard_map/ppermute | solution.py:329
  163.7 4.1 %collective-permute-start.35 = (f32[80,128]{1,0:T(8,128)S(1)}, f32[80,128]{1,0:T(8,128)S(1)}, u32[]{:S(2)}, u32[]{:S(2)}) collective-permute-start(f32[80,128]{1,0:T(8,128)S(1)} %add_add_fusion), channel_id=1, source_target_pairs={{0,6},{2,4},{4,2},{6,0},{1,7},{3,5},{5,3},{7,1},{8,14},{10,12},{12... | collective-permute-start | bytes 122888 | tf_op jit(solution)/shard_map/ppermute | solution.py:329
  165.5 4.4 %collective-permute-start.34 = (f32[80,128]{1,0:T(8,128)S(1)}, f32[80,128]{1,0:T(8,128)S(1)}, u32[]{:S(2)}, u32[]{:S(2)}) collective-permute-start(f32[80,128]{1,0:T(8,128)S(1)} %add_add_fusion), channel_id=1, source_target_pairs={{0,4},{2,6},{4,0},{6,2},{1,5},{3,7},{5,1},{7,3},{8,12},{10,14},{12... | collective-permute-start | bytes 122888 | tf_op jit(solution)/shard_map/ppermute | solution.py:329
  166.3 3.5 %collective-permute-start.33 = (f32[80,128]{1,0:T(8,128)S(1)}, f32[80,128]{1,0:T(8,128)S(1)}, u32[]{:S(2)}, u32[]{:S(2)}) collective-permute-start(f32[80,128]{1,0:T(8,128)S(1)} %add_add_fusion), channel_id=1, source_target_pairs={{0,2},{2,0},{4,6},{6,4},{1,3},{3,1},{5,7},{7,5},{8,10},{10,8},{12,... | collective-permute-start | bytes 122888 | tf_op jit(solution)/shard_map/ppermute | solution.py:329
  169.8 7.2 %copy-start.4 = (f32[4,80,128]{2,1,0:T(8,128)}, f32[4,80,128]{2,1,0:T(8,128)S(1)}, u32[]{:S(2)}) copy-start(f32[4,80,128]{2,1,0:T(8,128)S(1)} %pad_maximum_fusion.2.own_ref) | copy-start | bytes 491524
  169.9 7.2 %collective-permute-start.36 = (f32[4,80,128]{2,1,0:T(8,128)S(1)}, f32[4,80,128]{2,1,0:T(8,128)S(1)}, u32[]{:S(2)}, u32[]{:S(2)}) collective-permute-start(f32[4,80,128]{2,1,0:T(8,128)S(1)} %pad_maximum_fusion.2.own_ref), channel_id=1, source_target_pairs={{0,1},{1,0},{2,3},{3,2},{4,5},{5,4},{6,7},{7,6},{8,9},{9,8},{10,11... | collective-permute-start | bytes 491528 | tf_op jit(solution)/shard_map/ppermute | solution.py:329
  177.0 0.7 copy-start.7

commit v2 on v1

--- a/solution.py
+++ b/solution.py
@@ -198,8 +198,9 @@
             at = aligned(where_ref[p, s], SB)
             picked[:R, s * SB : (s + 1) * SB] = wide[0, :, at]
             picked[R:, s * SB : (s + 1) * SB] = wide[1, :, at]
-        by_real = bf16_dot(picked[...], near[p, :, 0].reshape(SLOTS * SB, SB))
-        by_imag = bf16_dot(picked[...], near[p, :, 1].reshape(SLOTS * SB, SB))
+        pair = [near[p, :, part].reshape(SLOTS * SB, SB) for part in range(2)]
+        both = bf16_dot(picked[...], jnp.concatenate(pair, axis=1))
+        by_real, by_imag = both[:, :SB], both[:, SB:]
         at = aligned(p, SB)
         x_real, x_imag = x[0, :, at], x[1, :, at]
         re, im = impedance[0:1, at], impedance[1:2, at]

time: 192 us -> 191 us (level)
  no operation moved by 1% of the time
where the time goes in v2:
time: 191 us
  starting transfers between devices  58.4 us (31%)
  Pallas kernels  49.3 us (26%)
  waiting for transfers between devices  37.4 us (20%)
  blocking collectives  37.3 us (20%)
  local copies, waits for them, and re-layouts  5.12 us (3%)
    pallas_call x7, Pallas kernels, call(): pl.pallas_call(kernel, out_shape=tuple((kind for kind, _ in out_specs)),...  49.3 us
    ppermute x33, starting transfers between devices, swap(): return lax.ppermute(x, axis, [(i, i ^ k) for i in range(n)])  48.7 us
    all_to_all x2, blocking collectives, gather_coeffs(): lax.all_to_all(products.reshape(8 * TILES, 16, 2 * K), ALL, 0, 0, tiled=T...  37.3 us
    ppermute x33, waiting for transfers between devices, swap(): return lax.ppermute(x, axis, [(i, i ^ k) for i in range(n)])  29 us
    ppermute x2, waiting for transfers between devices, operate(): from_right = lax.ppermute(low, ('z', 'c'), backward)  8.03 us
    ppermute x2, starting transfers between devices, operate(): from_left = lax.ppermute(high, ('z', 'c'), forward)  5.71 us
    unnamed x30, local copies, waits for them, and re-layouts  5.11 us
    ppermute x2, starting transfers between devices, operate(): from_right = lax.ppermute(low, ('z', 'c'), backward)  4.02 us
  transfers between devices with their start and end apart: 37, of which 29 were waited for; matrix products, arithmetic and copies ran while one was open for 0% of the time, Pallas kernels for 6%

profile of v2, /device:TPU:1, one launch (start us, length us, event | category | flops | bytes accessed | tf_op | source)
XLA Modules:
  0.0 190.5 jit_solution(2732845848222478984)
XLA Ops:
  0.7 1.1 copy-done
  1.9 1.4 shard_map.86
  3.2 1.5 collective-permute-start
  4.7 0.9 collective-permute-done
  5.5 3.9 %collective-permute-start.3 = (f32[64,128]{1,0:T(8,128)S(1)}, f32[64,128]{1,0:T(8,128)S(1)}, u32[]{:S(2)}, u32[]{:S(2)}) collective-permute-start(f32[64,128]{1,0:T(8,128)S(1)} %add.75), channel_id=1, source_target_pairs={{0,6},{2,4},{4,2},{6,0},{1,7},{3,5},{5,3},{7,1},{8,14},{10,12},{12... | collective-permute-start | bytes 98312 | tf_op jit(solution)/shard_map/ppermute | solution.py:330
  9.4 0.7 collective-permute-start.1
  10.7 3.0 %collective-permute-done.2 = f32[64,128]{1,0:T(8,128)S(1)} collective-permute-done((f32[64,128]{1,0:T(8,128)S(1)}, f32[64,128]{1,0:T(8,128)S(1)}, u32[]{:S(2)}, u32[]{:S(2)}) %collective-permute-start.2) | collective-permute-done | bytes 32800 | tf_op jit(solution)/shard_map/ppermute | solution.py:330
  13.7 2.8 %collective-permute-start.6 = (f32[64,128]{1,0:T(8,128)S(1)}, f32[64,128]{1,0:T(8,128)S(1)}, u32[]{:S(2)}, u32[]{:S(2)}) collective-permute-start(f32[64,128]{1,0:T(8,128)S(1)} %add_add_fusion.4), channel_id=1, source_target_pairs={{0,24},{8,16},{16,8},{24,0},{1,25},{9,17},{17,9},{25,1},{2,26},{10... | collective-permute-start | bytes 98312 | tf_op jit(solution)/shard_map/ppermute | solution.py:330
  17.8 3.0 %collective-permute-done.5 = f32[64,128]{1,0:T(8,128)S(1)} collective-permute-done((f32[64,128]{1,0:T(8,128)S(1)}, f32[64,128]{1,0:T(8,128)S(1)}, u32[]{:S(2)}, u32[]{:S(2)}) %collective-permute-start.5) | collective-permute-done | bytes 32800 | tf_op jit(solution)/shard_map/ppermute | solution.py:330
  20.8 2.6 %collective-permute-start.9 = (f32[64,128]{1,0:T(8,128)S(1)}, f32[64,128]{1,0:T(8,128)S(1)}, u32[]{:S(2)}, u32[]{:S(2)}) collective-permute-start(f32[64,128]{1,0:T(8,128)S(1)} %add_add_fusion.3), channel_id=1, source_target_pairs={{0,96},{32,64},{64,32},{96,0},{1,97},{33,65},{65,33},{97,1},{2,98}... | collective-permute-start | bytes 98312 | tf_op jit(solution)/shard_map/ppermute | solution.py:330
  24.1 0.7 collective-permute-done.9
  24.9 2.8 %collective-permute-done.8 = f32[64,128]{1,0:T(8,128)S(1)} collective-permute-done((f32[64,128]{1,0:T(8,128)S(1)}, f32[64,128]{1,0:T(8,128)S(1)}, u32[]{:S(2)}, u32[]{:S(2)}) %collective-permute-start.8) | collective-permute-done | bytes 32800 | tf_op jit(solution)/shard_map/ppermute | solution.py:330
  27.7 4.7 %collective-permute-start.10 = (f32[64,128]{1,0:T(8,128)S(1)}, f32[64,128]{1,0:T(8,128)S(1)}, u32[]{:S(2)}, u32[]{:S(2)}) collective-permute-start(f32[64,128]{1,0:T(8,128)S(1)} %add_add_fusion.2.mine_ref), channel_id=1, source_target_pairs={{0,1},{1,0},{2,3},{3,2},{4,5},{5,4},{6,7},{7,6},{8,9},{9,8},{10,11... | collective-permute-start | bytes 98312 | tf_op jit(solution)/shard_map/ppermute | solution.py:330
  32.4 0.9 collective-permute-done.10.other_ref
  33.8 8.6 %shard_map.87 = (f32[2,128,768]{2,1,0:T(8,128)}, bf16[2,128,768]{2,1,0:T(8,128)(2,1)}, bf16[2,128,256]{2,1,0:T(8,128)(2,1)}, bf16[2,128,256]{2,1,0:T(8,128)(2,1)}, bf16[16,128,128]{2,1,0:T(8,128)(2,1)}) custom-call(s32[3]{0:T(128)} %copy-done.1, f32[64,128]{1,0:T(8,128)} %copy-done.8, f32[64,128]{1,0:T(8,128)} %copy-done.13, f32[2,128,768]{2,1,0:T(8,128)} %side_ref.7, ...), custom_call_target="tpu_custom_call" | custom-call | flops 300000000 | bytes 6291456 | tf_op jit(solution)/shard_map/pallas_call | solution.py:396
  42.5 19.7 %all_to_all.10 = bf16[128,16,128]{2,1,0:T(8,128)(2,1)S(1)} all-to-all(bf16[128,16,128]{2,1,0:T(8,128)(2,1)} %bitcast.45), channel_id=1, replica_groups=mesh['x'=4,'y'=4,'z'=4,'c'=2] {'x','y','z','c'}, dimensions={0} | all-to-all | bytes 1048576 | tf_op jit(solution)/shard_map/all_to_all | solution.py:360
  62.2 0.9 collective-permute-start.13
  63.2 0.7 collective-permute-start.12
  63.8 1.7 collective-permute-start.11
  65.6 1.1 collective-permute-done.13
  66.6 1.1 collective-permute-done.12
  68.3 2.5 %collective-permute-start.14 = (bf16[4,16,16,128]{3,2,1,0:T(8,128)(2,1)S(1)}, bf16[4,16,16,128]{3,2,1,0:T(8,128)(2,1)S(1)}, u32[]{:S(2)}, u32[]{:S(2)}) collective-permute-start(bf16[4,16,16,128]{3,2,1,0:T(8,128)(2,1)S(1)} %pad_maximum_fusion.own_ref), channel_id=1, source_target_pairs={{0,1},{1,0},{2,3},{3,2},{4,5},{5,4},{6,7},{7,6},{8,9},{9,8},{10,11... | collective-permute-start | bytes 786440 | tf_op jit(solution)/shard_map/ppermute | solution.py:330
  70.7 2.9 %collective-permute-start.15 = (bf16[2,128,256]{2,1,0:T(8,128)(2,1)}, bf16[2,128,256]{2,1,0:T(8,128)(2,1)S(1)}, u32[]{:S(2)}, u32[]{:S(2)}) collective-permute-start(bf16[2,128,256]{2,1,0:T(8,128)(2,1)} %get-tuple-element.22), channel_id=1, source_target_pairs={{0,1},{1,2},{2,3},{3,4},{4,5},{5,6},{6,7},{8,9},{9,10},{10,11},{11... | collective-permute-start | bytes 393224 | tf_op jit(solution)/shard_map/ppermute | solution.py:408
  73.6 2.1 %collective-permute-start.16 = (bf16[2,128,256]{2,1,0:T(8,128)(2,1)}, bf16[2,128,256]{2,1,0:T(8,128)(2,1)S(1)}, u32[]{:S(2)}, u32[]{:S(2)}) collective-permute-start(bf16[2,128,256]{2,1,0:T(8,128)(2,1)} %get-tuple-element.23), channel_id=1, source_target_pairs={{1,0},{2,1},{3,2},{4,3},{5,4},{6,5},{7,6},{9,8},{10,9},{11,10},{12... | collective-permute-start | bytes 393224 | tf_op jit(solution)/shard_map/ppermute | solution.py:407
  76.3 3.8 %collective-permute-done.16.high_ref = bf16[2,128,256]{2,1,0:T(8,128)(2,1)S(1)} collective-permute-done((bf16[2,128,256]{2,1,0:T(8,128)(2,1)}, bf16[2,128,256]{2,1,0:T(8,128)(2,1)S(1)}, u32[]{:S(2)}, u32[]{:S(2)}) %collective-permute-start.16) | collective-permute-done | bytes 131104 | tf_op jit(solution)/shard_map/ppermute | solution.py:407
  80.8 5.5 %shard_map.88.base_ref = f32[2,128,768]{2,1,0:T(8,128)} custom-call(s32[6,6]{1,0:T(8,128)} %fusion.3.where_ref, f32[2,128,768]{2,1,0:T(8,128)} %get-tuple-element.20.x_ref.basis_0_ref, bf16[2,128,768]{2,1,0:T(8,128)(2,1)} %get-tuple-element.21.rounded_ref, bf16[2,128,256]{2,1,0:T(8,128)(2,1)} %copy-done.9, bf16[2,128,256]{2,1,0:T(8,128)(2,1)} %copy-done.11, ...), custom_call_target="tpu_custom_call" | custom-call | flops 300000000 | bytes 6291456 | tf_op jit(solution)/shard_map/pallas_call | solution.py:396
  86.3 0.7 copy-done.5
  87.0 6.4 %shard_map.89 = (f32[2,128,768]{2,1,0:T(8,128)}, bf16[2,128,768]{2,1,0:T(8,128)(2,1)}, bf16[2,128,256]{2,1,0:T(8,128)(2,1)}, bf16[2,128,256]{2,1,0:T(8,128)(2,1)}, bf16[16,128,128]{2,1,0:T(8,128)(2,1)}) custom-call(s32[3]{0:T(128)} %copy-done.1, s32[16,16]{1,0:T(8,128)} %ranks_ref.3, bf16[4,16,16,128]{3,2,1,0:T(8,128)(2,1)} %copy-done.2, ...), custom_call_target="tpu_custom_call" | custom-call | flops 300000000 | bytes 6291456 | tf_op jit(solution)/shard_map/pallas_call | solution.py:396
  93.5 17.6 %all_to_all.11 = bf16[128,16,128]{2,1,0:T(8,128)(2,1)S(1)} all-to-all(bf16[128,16,128]{2,1,0:T(8,128)(2,1)} %bitcast.44), channel_id=1, replica_groups=mesh['x'=4,'y'=4,'z'=4,'c'=2] {'x','y','z','c'}, dimensions={0} | all-to-all | bytes 1048576 | tf_op jit(solution)/shard_map/all_to_all | solution.py:360
  111.2 0.9 collective-permute-start.19
  112.1 0.7 collective-permute-start.18
  112.8 1.7 collective-permute-start.17
  114.5 1.1 collective-permute-done.19
  115.6 1.1 collective-permute-done.18
  117.2 2.5 %collective-permute-start.20 = (bf16[4,16,16,128]{3,2,1,0:T(8,128)(2,1)S(1)}, bf16[4,16,16,128]{3,2,1,0:T(8,128)(2,1)S(1)}, u32[]{:S(2)}, u32[]{:S(2)}) collective-permute-start(bf16[4,16,16,128]{3,2,1,0:T(8,128)(2,1)S(1)} %pad_maximum_fusion.1.own_ref), channel_id=1, source_target_pairs={{0,1},{1,0},{2,3},{3,2},{4,5},{5,4},{6,7},{7,6},{8,9},{9,8},{10,11... | collective-permute-start | bytes 786440 | tf_op jit(solution)/shard_map/ppermute | solution.py:330
  119.7 2.9 %collective-permute-start.21 = (bf16[2,128,256]{2,1,0:T(8,128)(2,1)}, bf16[2,128,256]{2,1,0:T(8,128)(2,1)S(1)}, u32[]{:S(2)}, u32[]{:S(2)}) collective-permute-start(bf16[2,128,256]{2,1,0:T(8,128)(2,1)} %get-tuple-element.27), channel_id=1, source_target_pairs={{0,1},{1,2},{2,3},{3,4},{4,5},{5,6},{6,7},{8,9},{9,10},{10,11},{11... | collective-permute-start | bytes 393224 | tf_op jit(solution)/shard_map/ppermute | solution.py:408
  122.5 1.9 %collective-permute-start.22 = (bf16[2,128,256]{2,1,0:T(8,128)(2,1)}, bf16[2,128,256]{2,1,0:T(8,128)(2,1)S(1)}, u32[]{:S(2)}, u32[]{:S(2)}) collective-permute-start(bf16[2,128,256]{2,1,0:T(8,128)(2,1)} %get-tuple-element.28), channel_id=1, source_target_pairs={{1,0},{2,1},{3,2},{4,3},{5,4},{6,5},{7,6},{9,8},{10,9},{11,10},{12... | collective-permute-start | bytes 393224 | tf_op jit(solution)/shard_map/ppermute | solution.py:407
  124.8 4.3 %collective-permute-done.22.high_ref = bf16[2,128,256]{2,1,0:T(8,128)(2,1)S(1)} collective-permute-done((bf16[2,128,256]{2,1,0:T(8,128)(2,1)}, bf16[2,128,256]{2,1,0:T(8,128)(2,1)S(1)}, u32[]{:S(2)}, u32[]{:S(2)}) %collective-permute-start.22) | collective-permute-done | bytes 131104 | tf_op jit(solution)/shard_map/ppermute | solution.py:407
  129.7 5.5 %shard_map.90.base_ref = f32[2,128,768]{2,1,0:T(8,128)} custom-call(s32[6,6]{1,0:T(8,128)} %fusion.3.where_ref, f32[2,128,768]{2,1,0:T(8,128)} %get-tuple-element.25.x_ref.basis_1_ref, bf16[2,128,768]{2,1,0:T(8,128)(2,1)} %get-tuple-element.26.rounded_ref, bf16[2,128,256]{2,1,0:T(8,128)(2,1)} %copy-done.10, bf16[2,128,256]{2,1,0:T(8,128)(2,1)} %copy-done.12, ...), custom_call_target="tpu_custom_call" | custom-call | flops 300000000 | bytes 6291456 | tf_op jit(solution)/shard_map/pallas_call | solution.py:396
  135.3 0.7 copy-done.6
  135.9 8.1 %shard_map.91 = (f32[2,128,768]{2,1,0:T(8,128)}, f32[4,80,128]{2,1,0:T(8,128)}, f32[4,80,128]{2,1,0:T(8,128)}) custom-call(s32[3]{0:T(128)} %copy-done.1, s32[16,16]{1,0:T(8,128)} %ranks_ref.3, bf16[4,16,16,128]{3,2,1,0:T(8,128)(2,1)} %copy-done.3, bf16[4,16,16,128]{3,2,1,0:T(8,128)(2,1)} %copy-done.6, bf16[2048,768]{1,0:T(8,128)(2,1)} %bitcast.41, ...), custom_call_target="tpu_custom_call" | custom-call | flops 300000000 | bytes 6291456 | tf_op jit(solution)/shard_map/pallas_call | solution.py:396
  144.1 1.6 collective-permute-done.23
  145.7 0.9 add.89
  147.2 1.5 collective-permute-start.25
  148.7 1.3 collective-permute-start.24
  150.0 0.8 collective-permute-done.26
  150.8 0.8 collective-permute-done.25
  152.5 1.9 collective-permute-start.28
  154.3 1.2 collective-permute-start.27
  155.5 0.8 collective-permute-done.29
  157.3 0.9 collective-permute-start.32
  158.3 1.3 collective-permute-start.31
  159.5 1.1 collective-permute-start.30
  160.7 0.8 collective-permute-done.32
  161.5 1.2 collective-permute-done.31
  162.7 1.7 collective-permute-start.35
  164.4 0.9 collective-permute-start.34
  165.3 0.7 collective-permute-start.33
  166.0 0.8 collective-permute-done.35
  166.8 2.0 %collective-permute-done.34 = f32[80,128]{1,0:T(8,128)S(1)} collective-permute-done((f32[80,128]{1,0:T(8,128)S(1)}, f32[80,128]{1,0:T(8,128)S(1)}, u32[]{:S(2)}, u32[]{:S(2)}) %collective-permute-start.34) | collective-permute-done | bytes 40992 | tf_op jit(solution)/shard_map/ppermute | solution.py:330
  168.8 6.1 %collective-permute-start.36 = (f32[4,80,128]{2,1,0:T(8,128)S(1)}, f32[4,80,128]{2,1,0:T(8,128)S(1)}, u32[]{:S(2)}, u32[]{:S(2)}) collective-permute-start(f32[4,80,128]{2,1,0:T(8,128)S(1)} %pad_maximum_fusion.2.own_ref), channel_id=1, source_target_pairs={{0,1},{1,0},{2,3},{3,2},{4,5},{5,4},{6,7},{7,6},{8,9},{9,8},{10,11... | collective-permute-start | bytes 491528 | tf_op jit(solution)/shard_map/ppermute | solution.py:330
  174.9 1.0 collective-permute-done.36.partner_ref
  176.0 0.7 copy-done.7
  176.6 13.7 %shard_map.92 = (f32[2,128,768]{2,1,0:T(8,128)}, f32[2,128,768]{2,1,0:T(8,128)}) custom-call(s32[3]{0:T(128)} %copy-done.1, f32[4,80,128]{2,1,0:T(8,128)} %copy-done.4, f32[4,80,128]{2,1,0:T(8,128)} %copy-done.7, f32[2,128,768]{2,1,0:T(8,128)} %side_ref.7, f32[2,128,768]{2,1,0:T(8,128)} %get-tuple-element.20.x_ref.basis_0_ref, ...), custom_call_target="tpu_custom_call" | custom-call | flops 300000000 | bytes 6291456 | tf_op jit(solution)/shard_map/pallas_call | solution.py:396
  (65 shorter events, 9.2 us)
Async XLA Ops:
  0.7 1.1 copy-start
  1.8 31.4 %copy-start.1 = (s32[3]{0:T(128)}, s32[3]{0:T(128)S(1)}, u32[]{:S(2)}) copy-start(s32[3]{0:T(128)S(1)} %pad_add_fusion.place_ref) | copy-start | bytes 40
  3.2 2.3 %collective-permute-start = (f32[64,128]{1,0:T(8,128)S(1)}, f32[64,128]{1,0:T(8,128)S(1)}, u32[]{:S(2)}, u32[]{:S(2)}) collective-permute-start(f32[64,128]{1,0:T(8,128)S(1)} %get-tuple-element.18), channel_id=1, source_target_pairs={{0,1},{1,0},{2,3},{3,2},{4,5},{5,4},{6,7},{7,6},{8,9},{9,8},{10,11... | collective-permute-start | bytes 98312 | tf_op jit(solution)/shard_map/ppermute | solution.py:330
  5.5 5.2 %collective-permute-start.3 = (f32[64,128]{1,0:T(8,128)S(1)}, f32[64,128]{1,0:T(8,128)S(1)}, u32[]{:S(2)}, u32[]{:S(2)}) collective-permute-start(f32[64,128]{1,0:T(8,128)S(1)} %add.75), channel_id=1, source_target_pairs={{0,6},{2,4},{4,2},{6,0},{1,7},{3,5},{5,3},{7,1},{8,14},{10,12},{12... | collective-permute-start | bytes 98312 | tf_op jit(solution)/shard_map/ppermute | solution.py:330
  9.4 4.3 %collective-permute-start.2 = (f32[64,128]{1,0:T(8,128)S(1)}, f32[64,128]{1,0:T(8,128)S(1)}, u32[]{:S(2)}, u32[]{:S(2)}) collective-permute-start(f32[64,128]{1,0:T(8,128)S(1)} %add.75), channel_id=1, source_target_pairs={{0,4},{2,6},{4,0},{6,2},{1,5},{3,7},{5,1},{7,3},{8,12},{10,14},{12... | collective-permute-start | bytes 98312 | tf_op jit(solution)/shard_map/ppermute | solution.py:330
  9.4 4.3 %collective-permute-start.1 = (f32[64,128]{1,0:T(8,128)S(1)}, f32[64,128]{1,0:T(8,128)S(1)}, u32[]{:S(2)}, u32[]{:S(2)}) collective-permute-start(f32[64,128]{1,0:T(8,128)S(1)} %add.75), channel_id=1, source_target_pairs={{0,2},{2,0},{4,6},{6,4},{1,3},{3,1},{5,7},{7,5},{8,10},{10,8},{12,... | collective-permute-start | bytes 98312 | tf_op jit(solution)/shard_map/ppermute | solution.py:330
  13.7 4.1 %collective-permute-start.6 = (f32[64,128]{1,0:T(8,128)S(1)}, f32[64,128]{1,0:T(8,128)S(1)}, u32[]{:S(2)}, u32[]{:S(2)}) collective-permute-start(f32[64,128]{1,0:T(8,128)S(1)} %add_add_fusion.4), channel_id=1, source_target_pairs={{0,24},{8,16},{16,8},{24,0},{1,25},{9,17},{17,9},{25,1},{2,26},{10... | collective-permute-start | bytes 98312 | tf_op jit(solution)/shard_map/ppermute | solution.py:330
  16.5 4.3 %collective-permute-start.5 = (f32[64,128]{1,0:T(8,128)S(1)}, f32[64,128]{1,0:T(8,128)S(1)}, u32[]{:S(2)}, u32[]{:S(2)}) collective-permute-start(f32[64,128]{1,0:T(8,128)S(1)} %add_add_fusion.4), channel_id=1, source_target_pairs={{0,16},{8,24},{16,0},{24,8},{1,17},{9,25},{17,1},{25,9},{2,18},{10... | collective-permute-start | bytes 98312 | tf_op jit(solution)/shard_map/ppermute | solution.py:330
  16.9 3.9 %collective-permute-start.4 = (f32[64,128]{1,0:T(8,128)S(1)}, f32[64,128]{1,0:T(8,128)S(1)}, u32[]{:S(2)}, u32[]{:S(2)}) collective-permute-start(f32[64,128]{1,0:T(8,128)S(1)} %add_add_fusion.4), channel_id=1, source_target_pairs={{0,8},{8,0},{16,24},{24,16},{1,9},{9,1},{17,25},{25,17},{2,10},{10... | collective-permute-start | bytes 98312 | tf_op jit(solution)/shard_map/ppermute | solution.py:330
  20.8 54.9 %copy-start.14 = (s32[1,6,6]{2,0,1:T(1,128)S(1)}, s32[1,6,6]{2,0,1:T(1,128)}, u32[]{:S(2)}) copy-start(s32[1,6,6]{2,0,1:T(1,128)} %param.10) | copy-start | bytes 436
  20.8 4.1 %collective-permute-start.9 = (f32[64,128]{1,0:T(8,128)S(1)}, f32[64,128]{1,0:T(8,128)S(1)}, u32[]{:S(2)}, u32[]{:S(2)}) collective-permute-start(f32[64,128]{1,0:T(8,128)S(1)} %add_add_fusion.3), channel_id=1, source_target_pairs={{0,96},{32,64},{64,32},{96,0},{1,97},{33,65},{65,33},{97,1},{2,98}... | collective-permute-start | bytes 98312 | tf_op jit(solution)/shard_map/ppermute | solution.py:330
  23.4 4.3 %collective-permute-start.8 = (f32[64,128]{1,0:T(8,128)S(1)}, f32[64,128]{1,0:T(8,128)S(1)}, u32[]{:S(2)}, u32[]{:S(2)}) collective-permute-start(f32[64,128]{1,0:T(8,128)S(1)} %add_add_fusion.3), channel_id=1, source_target_pairs={{0,64},{32,96},{64,0},{96,32},{1,65},{33,97},{65,1},{97,33},{2,66}... | collective-permute-start | bytes 98312 | tf_op jit(solution)/shard_map/ppermute | solution.py:330
  23.9 3.8 %collective-permute-start.7 = (f32[64,128]{1,0:T(8,128)S(1)}, f32[64,128]{1,0:T(8,128)S(1)}, u32[]{:S(2)}, u32[]{:S(2)}) collective-permute-start(f32[64,128]{1,0:T(8,128)S(1)} %add_add_fusion.3), channel_id=1, source_target_pairs={{0,32},{32,0},{64,96},{96,64},{1,33},{33,1},{65,97},{97,65},{2,34}... | collective-permute-start | bytes 98312 | tf_op jit(solution)/shard_map/ppermute | solution.py:330
  27.6 5.6 %copy-start.8 = (f32[64,128]{1,0:T(8,128)}, f32[64,128]{1,0:T(8,128)S(1)}, u32[]{:S(2)}) copy-start(f32[64,128]{1,0:T(8,128)S(1)} %add_add_fusion.2.mine_ref) | copy-start | bytes 98308
  27.7 5.6 %collective-permute-start.10 = (f32[64,128]{1,0:T(8,128)S(1)}, f32[64,128]{1,0:T(8,128)S(1)}, u32[]{:S(2)}, u32[]{:S(2)}) collective-permute-start(f32[64,128]{1,0:T(8,128)S(1)} %add_add_fusion.2.mine_ref), channel_id=1, source_target_pairs={{0,1},{1,0},{2,3},{3,2},{4,5},{5,4},{6,7},{7,6},{8,9},{9,8},{10,11... | collective-permute-start | bytes 98312 | tf_op jit(solution)/shard_map/ppermute | solution.py:330
  33.2 0.6 copy-start.13
  62.2 4.4 %collective-permute-start.13 = (bf16[16,16,128]{2,1,0:T(8,128)(2,1)S(1)}, bf16[16,16,128]{2,1,0:T(8,128)(2,1)S(1)}, u32[]{:S(2)}, u32[]{:S(2)}) collective-permute-start(bf16[16,16,128]{2,1,0:T(8,128)(2,1)S(1)} %bitcast_reduce_fusion.1), channel_id=1, source_target_pairs={{0,6},{2,4},{4,2},{6,0},{1,7},{3,5},{5,3},{7,1},{8,14},{10,12},{12... | collective-permute-start | bytes 196616 | tf_op jit(solution)/shard_map/ppermute | solution.py:330
  63.2 4.6 %collective-permute-start.12 = (bf16[16,16,128]{2,1,0:T(8,128)(2,1)S(1)}, bf16[16,16,128]{2,1,0:T(8,128)(2,1)S(1)}, u32[]{:S(2)}, u32[]{:S(2)}) collective-permute-start(bf16[16,16,128]{2,1,0:T(8,128)(2,1)S(1)} %bitcast_reduce_fusion.1), channel_id=1, source_target_pairs={{0,4},{2,6},{4,0},{6,2},{1,5},{3,7},{5,1},{7,3},{8,12},{10,14},{12... | collective-permute-start | bytes 196616 | tf_op jit(solution)/shard_map/ppermute | solution.py:330
  63.8 4.4 %collective-permute-start.11 = (bf16[16,16,128]{2,1,0:T(8,128)(2,1)S(1)}, bf16[16,16,128]{2,1,0:T(8,128)(2,1)S(1)}, u32[]{:S(2)}, u32[]{:S(2)}) collective-permute-start(bf16[16,16,128]{2,1,0:T(8,128)(2,1)S(1)} %bitcast_reduce_fusion.1), channel_id=1, source_target_pairs={{0,2},{2,0},{4,6},{6,4},{1,3},{3,1},{5,7},{7,5},{8,10},{10,8},{12,... | collective-permute-start | bytes 196616 | tf_op jit(solution)/shard_map/ppermute | solution.py:330
  68.3 18.1 %copy-start.2 = (bf16[4,16,16,128]{3,2,1,0:T(8,128)(2,1)}, bf16[4,16,16,128]{3,2,1,0:T(8,128)(2,1)S(1)}, u32[]{:S(2)}) copy-start(bf16[4,16,16,128]{3,2,1,0:T(8,128)(2,1)S(1)} %pad_maximum_fusion.own_ref) | copy-start | bytes 786436
  68.3 18.0 %collective-permute-start.14 = (bf16[4,16,16,128]{3,2,1,0:T(8,128)(2,1)S(1)}, bf16[4,16,16,128]{3,2,1,0:T(8,128)(2,1)S(1)}, u32[]{:S(2)}, u32[]{:S(2)}) collective-permute-start(bf16[4,16,16,128]{3,2,1,0:T(8,128)(2,1)S(1)} %pad_maximum_fusion.own_ref), channel_id=1, source_target_pairs={{0,1},{1,0},{2,3},{3,2},{4,5},{5,4},{6,7},{7,6},{8,9},{9,8},{10,11... | collective-permute-start | bytes 786440 | tf_op jit(solution)/shard_map/ppermute | solution.py:330
  70.7 5.6 %collective-permute-start.15 = (bf16[2,128,256]{2,1,0:T(8,128)(2,1)}, bf16[2,128,256]{2,1,0:T(8,128)(2,1)S(1)}, u32[]{:S(2)}, u32[]{:S(2)}) collective-permute-start(bf16[2,128,256]{2,1,0:T(8,128)(2,1)} %get-tuple-element.22), channel_id=1, source_target_pairs={{0,1},{1,2},{2,3},{3,4},{4,5},{5,6},{6,7},{8,9},{9,10},{10,11},{11... | collective-permute-start | bytes 393224 | tf_op jit(solution)/shard_map/ppermute | solution.py:408
  73.6 6.5 %collective-permute-start.16 = (bf16[2,128,256]{2,1,0:T(8,128)(2,1)}, bf16[2,128,256]{2,1,0:T(8,128)(2,1)S(1)}, u32[]{:S(2)}, u32[]{:S(2)}) collective-permute-start(bf16[2,128,256]{2,1,0:T(8,128)(2,1)} %get-tuple-element.23), channel_id=1, source_target_pairs={{1,0},{2,1},{3,2},{4,3},{5,4},{6,5},{7,6},{9,8},{10,9},{11,10},{12... | collective-permute-start | bytes 393224 | tf_op jit(solution)/shard_map/ppermute | solution.py:407
  76.3 3.8 %copy-start.9 = (bf16[2,128,256]{2,1,0:T(8,128)(2,1)}, bf16[2,128,256]{2,1,0:T(8,128)(2,1)S(1)}, u32[]{:S(2)}) copy-start(bf16[2,128,256]{2,1,0:T(8,128)(2,1)S(1)} %collective-permute-done.15.low_ref) | copy-start | bytes 393220
  80.1 0.6 copy-start.11
  86.3 0.7 copy-start.5
  111.2 4.4 %collective-permute-start.19 = (bf16[16,16,128]{2,1,0:T(8,128)(2,1)S(1)}, bf16[16,16,128]{2,1,0:T(8,128)(2,1)S(1)}, u32[]{:S(2)}, u32[]{:S(2)}) collective-permute-start(bf16[16,16,128]{2,1,0:T(8,128)(2,1)S(1)} %bitcast_reduce_fusion), channel_id=1, source_target_pairs={{0,6},{2,4},{4,2},{6,0},{1,7},{3,5},{5,3},{7,1},{8,14},{10,12},{12... | collective-permute-start | bytes 196616 | tf_op jit(solution)/shard_map/ppermute | solution.py:330
  112.1 4.6 %collective-permute-start.18 = (bf16[16,16,128]{2,1,0:T(8,128)(2,1)S(1)}, bf16[16,16,128]{2,1,0:T(8,128)(2,1)S(1)}, u32[]{:S(2)}, u32[]{:S(2)}) collective-permute-start(bf16[16,16,128]{2,1,0:T(8,128)(2,1)S(1)} %bitcast_reduce_fusion), channel_id=1, source_target_pairs={{0,4},{2,6},{4,0},{6,2},{1,5},{3,7},{5,1},{7,3},{8,12},{10,14},{12... | collective-permute-start | bytes 196616 | tf_op jit(solution)/shard_map/ppermute | solution.py:330
  112.8 4.4 %collective-permute-start.17 = (bf16[16,16,128]{2,1,0:T(8,128)(2,1)S(1)}, bf16[16,16,128]{2,1,0:T(8,128)(2,1)S(1)}, u32[]{:S(2)}, u32[]{:S(2)}) collective-permute-start(bf16[16,16,128]{2,1,0:T(8,128)(2,1)S(1)} %bitcast_reduce_fusion), channel_id=1, source_target_pairs={{0,2},{2,0},{4,6},{6,4},{1,3},{3,1},{5,7},{7,5},{8,10},{10,8},{12,... | collective-permute-start | bytes 196616 | tf_op jit(solution)/shard_map/ppermute | solution.py:330
  117.2 18.0 %copy-start.3 = (bf16[4,16,16,128]{3,2,1,0:T(8,128)(2,1)}, bf16[4,16,16,128]{3,2,1,0:T(8,128)(2,1)S(1)}, u32[]{:S(2)}) copy-start(bf16[4,16,16,128]{3,2,1,0:T(8,128)(2,1)S(1)} %pad_maximum_fusion.1.own_ref) | copy-start | bytes 786436
  117.2 18.0 %collective-permute-start.20 = (bf16[4,16,16,128]{3,2,1,0:T(8,128)(2,1)S(1)}, bf16[4,16,16,128]{3,2,1,0:T(8,128)(2,1)S(1)}, u32[]{:S(2)}, u32[]{:S(2)}) collective-permute-start(bf16[4,16,16,128]{3,2,1,0:T(8,128)(2,1)S(1)} %pad_maximum_fusion.1.own_ref), channel_id=1, source_target_pairs={{0,1},{1,0},{2,3},{3,2},{4,5},{5,4},{6,7},{7,6},{8,9},{9,8},{10,11... | collective-permute-start | bytes 786440 | tf_op jit(solution)/shard_map/ppermute | solution.py:330
  119.7 5.1 %collective-permute-start.21 = (bf16[2,128,256]{2,1,0:T(8,128)(2,1)}, bf16[2,128,256]{2,1,0:T(8,128)(2,1)S(1)}, u32[]{:S(2)}, u32[]{:S(2)}) collective-permute-start(bf16[2,128,256]{2,1,0:T(8,128)(2,1)} %get-tuple-element.27), channel_id=1, source_target_pairs={{0,1},{1,2},{2,3},{3,4},{4,5},{5,6},{6,7},{8,9},{9,10},{10,11},{11... | collective-permute-start | bytes 393224 | tf_op jit(solution)/shard_map/ppermute | solution.py:408
  122.5 6.5 %collective-permute-start.22 = (bf16[2,128,256]{2,1,0:T(8,128)(2,1)}, bf16[2,128,256]{2,1,0:T(8,128)(2,1)S(1)}, u32[]{:S(2)}, u32[]{:S(2)}) collective-permute-start(bf16[2,128,256]{2,1,0:T(8,128)(2,1)} %get-tuple-element.28), channel_id=1, source_target_pairs={{1,0},{2,1},{3,2},{4,3},{5,4},{6,5},{7,6},{9,8},{10,9},{11,10},{12... | collective-permute-start | bytes 393224 | tf_op jit(solution)/shard_map/ppermute | solution.py:407
  124.8 4.3 %copy-start.10 = (bf16[2,128,256]{2,1,0:T(8,128)(2,1)}, bf16[2,128,256]{2,1,0:T(8,128)(2,1)S(1)}, u32[]{:S(2)}) copy-start(bf16[2,128,256]{2,1,0:T(8,128)(2,1)S(1)} %collective-permute-done.21.low_ref) | copy-start | bytes 393220
  129.0 0.7 copy-start.12
  135.3 0.7 copy-start.6
  144.1 1.7 collective-permute-start.23
  146.7 4.1 %collective-permute-start.26 = (f32[80,128]{1,0:T(8,128)S(1)}, f32[80,128]{1,0:T(8,128)S(1)}, u32[]{:S(2)}, u32[]{:S(2)}) collective-permute-start(f32[80,128]{1,0:T(8,128)S(1)} %get-tuple-element.32), channel_id=1, source_target_pairs={{0,6},{2,4},{4,2},{6,0},{1,7},{3,5},{5,3},{7,1},{8,14},{10,12},{12... | collective-permute-start | bytes 122888 | tf_op jit(solution)/shard_map/ppermute | solution.py:330
  147.2 4.5 %collective-permute-start.25 = (f32[80,128]{1,0:T(8,128)S(1)}, f32[80,128]{1,0:T(8,128)S(1)}, u32[]{:S(2)}, u32[]{:S(2)}) collective-permute-start(f32[80,128]{1,0:T(8,128)S(1)} %get-tuple-element.33), channel_id=1, source_target_pairs={{0,4},{2,6},{4,0},{6,2},{1,5},{3,7},{5,1},{7,3},{8,12},{10,14},{12... | collective-permute-start | bytes 122888 | tf_op jit(solution)/shard_map/ppermute | solution.py:330
  148.7 3.5 %collective-permute-start.24 = (f32[80,128]{1,0:T(8,128)S(1)}, f32[80,128]{1,0:T(8,128)S(1)}, u32[]{:S(2)}, u32[]{:S(2)}) collective-permute-start(f32[80,128]{1,0:T(8,128)S(1)} %get-tuple-element.34), channel_id=1, source_target_pairs={{0,2},{2,0},{4,6},{6,4},{1,3},{3,1},{5,7},{7,5},{8,10},{10,8},{12,... | collective-permute-start | bytes 122888 | tf_op jit(solution)/shard_map/ppermute | solution.py:330
  152.2 4.1 %collective-permute-start.29 = (f32[80,128]{1,0:T(8,128)S(1)}, f32[80,128]{1,0:T(8,128)S(1)}, u32[]{:S(2)}, u32[]{:S(2)}) collective-permute-start(f32[80,128]{1,0:T(8,128)S(1)} %fusion.1), channel_id=1, source_target_pairs={{0,24},{8,16},{16,8},{24,0},{1,25},{9,17},{17,9},{25,1},{2,26},{10... | collective-permute-start | bytes 122888 | tf_op jit(solution)/shard_map/ppermute | solution.py:330
  152.5 4.4 %collective-permute-start.28 = (f32[80,128]{1,0:T(8,128)S(1)}, f32[80,128]{1,0:T(8,128)S(1)}, u32[]{:S(2)}, u32[]{:S(2)}) collective-permute-start(f32[80,128]{1,0:T(8,128)S(1)} %fusion.1), channel_id=1, source_target_pairs={{0,16},{8,24},{16,0},{24,8},{1,17},{9,25},{17,1},{25,9},{2,18},{10... | collective-permute-start | bytes 122888 | tf_op jit(solution)/shard_map/ppermute | solution.py:330
  154.3 3.0 %collective-permute-start.27 = (f32[80,128]{1,0:T(8,128)S(1)}, f32[80,128]{1,0:T(8,128)S(1)}, u32[]{:S(2)}, u32[]{:S(2)}) collective-permute-start(f32[80,128]{1,0:T(8,128)S(1)} %fusion.1), channel_id=1, source_target_pairs={{0,8},{8,0},{16,24},{24,16},{1,9},{9,1},{17,25},{25,17},{2,10},{10... | collective-permute-start | bytes 122888 | tf_op jit(solution)/shard_map/ppermute | solution.py:330
  157.3 4.1 %collective-permute-start.32 = (f32[80,128]{1,0:T(8,128)S(1)}, f32[80,128]{1,0:T(8,128)S(1)}, u32[]{:S(2)}, u32[]{:S(2)}) collective-permute-start(f32[80,128]{1,0:T(8,128)S(1)} %add_add_fusion.1), channel_id=1, source_target_pairs={{0,96},{32,64},{64,32},{96,0},{1,97},{33,65},{65,33},{97,1},{2,98}... | collective-permute-start | bytes 122888 | tf_op jit(solution)/shard_map/ppermute | solution.py:330
  158.3 4.4 %collective-permute-start.31 = (f32[80,128]{1,0:T(8,128)S(1)}, f32[80,128]{1,0:T(8,128)S(1)}, u32[]{:S(2)}, u32[]{:S(2)}) collective-permute-start(f32[80,128]{1,0:T(8,128)S(1)} %add_add_fusion.1), channel_id=1, source_target_pairs={{0,64},{32,96},{64,0},{96,32},{1,65},{33,97},{65,1},{97,33},{2,66}... | collective-permute-start | bytes 122888 | tf_op jit(solution)/shard_map/ppermute | solution.py:330
  159.5 3.1 %collective-permute-start.30 = (f32[80,128]{1,0:T(8,128)S(1)}, f32[80,128]{1,0:T(8,128)S(1)}, u32[]{:S(2)}, u32[]{:S(2)}) collective-permute-start(f32[80,128]{1,0:T(8,128)S(1)} %add_add_fusion.1), channel_id=1, source_target_pairs={{0,32},{32,0},{64,96},{96,64},{1,33},{33,1},{65,97},{97,65},{2,34}... | collective-permute-start | bytes 122888 | tf_op jit(solution)/shard_map/ppermute | solution.py:330
  162.7 4.1 %collective-permute-start.35 = (f32[80,128]{1,0:T(8,128)S(1)}, f32[80,128]{1,0:T(8,128)S(1)}, u32[]{:S(2)}, u32[]{:S(2)}) collective-permute-start(f32[80,128]{1,0:T(8,128)S(1)} %add_add_fusion), channel_id=1, source_target_pairs={{0,6},{2,4},{4,2},{6,0},{1,7},{3,5},{5,3},{7,1},{8,14},{10,12},{12... | collective-permute-start | bytes 122888 | tf_op jit(solution)/shard_map/ppermute | solution.py:330
  164.4 4.4 %collective-permute-start.34 = (f32[80,128]{1,0:T(8,128)S(1)}, f32[80,128]{1,0:T(8,128)S(1)}, u32[]{:S(2)}, u32[]{:S(2)}) collective-permute-start(f32[80,128]{1,0:T(8,128)S(1)} %add_add_fusion), channel_id=1, source_target_pairs={{0,4},{2,6},{4,0},{6,2},{1,5},{3,7},{5,1},{7,3},{8,12},{10,14},{12... | collective-permute-start | bytes 122888 | tf_op jit(solution)/shard_map/ppermute | solution.py:330
  165.3 3.5 %collective-permute-start.33 = (f32[80,128]{1,0:T(8,128)S(1)}, f32[80,128]{1,0:T(8,128)S(1)}, u32[]{:S(2)}, u32[]{:S(2)}) collective-permute-start(f32[80,128]{1,0:T(8,128)S(1)} %add_add_fusion), channel_id=1, source_target_pairs={{0,2},{2,0},{4,6},{6,4},{1,3},{3,1},{5,7},{7,5},{8,10},{10,8},{12,... | collective-permute-start | bytes 122888 | tf_op jit(solution)/shard_map/ppermute | solution.py:330
  168.8 7.2 %copy-start.4 = (f32[4,80,128]{2,1,0:T(8,128)}, f32[4,80,128]{2,1,0:T(8,128)S(1)}, u32[]{:S(2)}) copy-start(f32[4,80,128]{2,1,0:T(8,128)S(1)} %pad_maximum_fusion.2.own_ref) | copy-start | bytes 491524
  168.8 7.2 %collective-permute-start.36 = (f32[4,80,128]{2,1,0:T(8,128)S(1)}, f32[4,80,128]{2,1,0:T(8,128)S(1)}, u32[]{:S(2)}, u32[]{:S(2)}) collective-permute-start(f32[4,80,128]{2,1,0:T(8,128)S(1)} %pad_maximum_fusion.2.own_ref), channel_id=1, source_target_pairs={{0,1},{1,0},{2,3},{3,2},{4,5},{5,4},{6,7},{7,6},{8,9},{9,8},{10,11... | collective-permute-start | bytes 491528 | tf_op jit(solution)/shard_map/ppermute | solution.py:330
  176.0 0.7 copy-start.7
